TPU v7x, 128 devices: a whole 4x4x4 slice. The times are simulated.
128 devices in a mesh: gx: 16 (over z, x), gy: 8 (over y, core).
Axes of the slice: x: 4, y: 4, z: 4, core: 2. Of those that a mesh axis runs over, the one named last changes fastest.
Arguments:
- field: float32 [32, 1024, 1024], P(None, 'gx', 'gy'), may hold values from -6 to 6
- conductivity: float32 [32, 1024, 1024], P(None, 'gx', 'gy'), may hold values from 0.2 to 1
- rate: float32 [32, 1024, 1024], P(None, 'gx', 'gy'), may hold values from 0.05 to 0.5
- patch_cell: int32 [32768], P(('gx', 'gy')), may hold values from 0 to 255
- trainer: int32 [32768, 1], P(('gx', 'gy')), may hold values from 0 to 127; in each aligned block of 256 rows (0 to 255, 256 to 511, ...) at most 4 rows name the same one
- res_slot: int32 [131072], P(('gx', 'gy')), may hold values from 0 to 2047
- reservoir: bfloat16 [262144, 2048], P(('gx', 'gy')), may hold values from -6 to 6
- weights: float32 [2, 1024, 1024], P(None, ('gx', 'gy')), may hold values from -0.1875 to 0.1875
- w_mom: float32 [2, 1024, 1024], P(None, ('gx', 'gy')), may hold values from -0.75 to 0.75
- w_var: float32 [2, 1024, 1024], P(None, ('gx', 'gy')), may hold values from 0.001 to 0.1
- biases: float32 [2, 1024], P(None, ('gx', 'gy')), may hold values from -6 to 6
- b_mom: float32 [2, 1024], P(None, ('gx', 'gy')), may hold values from -0.75 to 0.75
- b_var: float32 [2, 1024], P(None, ('gx', 'gy')), may hold values from 0.001 to 2
Outputs:
- new_field: float32 [32, 1024, 1024], P(None, 'gx', 'gy')
- new_weights: float32 [2, 1024, 1024], P(None, ('gx', 'gy'))
- new_w_mom: float32 [2, 1024, 1024], P(None, ('gx', 'gy'))
- new_w_var: float32 [2, 1024, 1024], P(None, ('gx', 'gy'))
- new_biases: float32 [2, 1024], P(None, ('gx', 'gy'))
- new_b_mom: float32 [2, 1024], P(None, ('gx', 'gy'))
- new_b_var: float32 [2, 1024], P(None, ('gx', 'gy'))
Inputs may be any that keep to these rules, and one draw needn't show every extreme that they name: At most 4 of the patches of one device go to one trainer. `res_slot`: slots of the trainer's own reservoir.
All inputs are finite; a program needn't handle non-finite values.
Results may differ from a plain program's by a relative error of at most 0.0003.
The roundings to bfloat16 on the way count: a program that leaves them out, or rounds other values in their place, can miss the bound.
Values may be sent and summed in bfloat16 or wider, within the bound.
No kernel may reach another device: no remote copies, remote signals or barrier semaphores. Data moves between devices by JAX's collectives and lax.ppermute only.
A program may use at most 128 MiB of HBM per device.

v0:
```python
import jax
import jax.numpy as jnp
from jax import lax
from jax.experimental import pallas as pl
from jax.experimental.pallas import tpu as pltpu
from jax.sharding import PartitionSpec as P


PW = 32
STEPS = 4
AXES = ("gx", "gy")

time_step = 0.15
learn_rate = 0.001
beta_one = 0.9
beta_two = 0.99
adam_count = 20
tiny_eps = 1e-08


def shift_pairs(axis):
    peers = lax.axis_size(axis)
    up = [(i, i + 1) for i in range(peers - 1)]
    return up, [(j, i) for i, j in up]


def exchange(first, last, axis):
    up, down = shift_pairs(axis)
    return lax.ppermute(first, axis, down), lax.ppermute(last, axis, up)


def lane_ids(shape):
    return lax.broadcasted_iota(jnp.int32, shape, len(shape) - 1)


def pack_kernel(u_ref, k_ref, r_ref, halo_ref, first_ref, last_ref):
    depth = u_ref.shape[0]
    slot = lane_ids((1, 128)) // STEPS
    for a, ref in enumerate((u_ref, k_ref, r_ref)):
        for part, rows in (("main", ref.shape[1]), ("halo", 2 * STEPS)):
            first = jnp.zeros((rows, 128), jnp.float32)
            last = first
            for z in range(depth):
                slab = ref[z] if part == "main" else halo_ref[a, z]
                turned = pltpu.roll(slab, z * STEPS, 1) if z else slab
                first = jnp.where(slot == z, turned, first)
                last = jnp.where(slot == (z - 1) % depth, turned, last)
            at = slice(0, rows) if part == "main" else slice(ref.shape[1], ref.shape[1] + rows)
            first_ref[a, at, :] = first
            last_ref[a, at, :] = last


def pack_sides(field, conductivity, rate, halo):
    rows = field.shape[1] + 2 * STEPS
    out = jax.ShapeDtypeStruct((3, rows, 128), jnp.float32)
    return pl.pallas_call(pack_kernel, out_shape=(out, out), name="pack_sides", cost_estimate=pl.CostEstimate(flops=1 << 24, bytes_accessed=12 << 20, transcendentals=0))(
        field, conductivity, rate, halo
    )


def table_rows(read, table_ref, level, depth):
    group = lane_ids((1, 128)) // PW
    per = 128 // PW

    def body(block, carry):
        slabs = [read(block * per + k) for k in range(per)]
        cells_x = slabs[0].shape[0]
        for yb in range(per):
            row = None
            for k in range(per):
                turn = (k - yb) % per * PW
                part = pltpu.roll(slabs[k], turn, 1) if turn else slabs[k]
                row = part if row is None else jnp.where(group == k, part, row)
            at = pl.multiple_of(level * depth * PW + block * 128, 128)
            table_ref[yb * cells_x : (yb + 1) * cells_x, pl.ds(at, 128)] = row.astype(jnp.bfloat16)
        return carry

    lax.fori_loop(0, depth // per, body, 0)


def solve_kernel(
    pos_ref,
    u_ref,
    k_ref,
    r_ref,
    halo_ref,
    right_ref,
    left_ref,
    out_ref,
    table_ref,
    ua,
    ub,
    kk,
    rr,
    cx,
    cy,
    cz,
    dt_ref,
):
    depth, cells_x, cells_y = u_ref.shape
    rows, lanes = cells_x + 2 * STEPS, 2 * cells_y
    lane = lane_ids((1, cells_y))
    blank = jnp.zeros((rows, lanes), jnp.float32)
    for ref in (ua, ub, kk):
        ref[0] = blank
        ref[depth + 1] = blank
    for z in range(depth):
        for a, (src, dst, at) in enumerate(((u_ref, ua, z + 1), (k_ref, kk, z + 1), (r_ref, rr, z))):
            dst[at, 0:cells_x, 0:cells_y] = src[z]
            dst[at, cells_x:rows, 0:cells_y] = halo_ref[a, z]
            turn = -z * STEPS % cells_y
            right, left = right_ref[a], left_ref[a]
            if turn:
                right, left = pltpu.roll(right, turn, 1), pltpu.roll(left, turn, 1)
            side = jnp.where(lane < STEPS, right, 0.0)
            side = jnp.where(lane >= cells_y - STEPS, left, side)
            dst[at, :, cells_y:lanes] = side

    def faces(z, carry):
        k = kk[z + 1]
        cz[z] = 0.5 * (kk[z] + k)
        cx[z] = 0.5 * (k + pltpu.roll(k, rows - 1, 0))
        cy[z] = 0.5 * (k + pltpu.roll(k, lanes - 1, 1))
        return carry

    lax.fori_loop(0, depth, faces, 0)
    cz[depth] = 0.5 * kk[depth]

    gx, gy = pos_ref[0], pos_ref[1]
    row_id = lax.broadcasted_iota(jnp.int32, (rows, lanes), 0)
    lane_id = lax.broadcasted_iota(jnp.int32, (rows, lanes), 1)
    below = jnp.where(gx < pos_ref[2] - 1, 1, 0)
    above = jnp.where(gx > 0, 1, 0)
    after = jnp.where(gy < pos_ref[3] - 1, 1, 0)
    before = jnp.where(gy > 0, 1, 0)
    row_in = jnp.where(row_id < cells_x, 1, jnp.where(row_id < cells_x + STEPS, below, above))
    lane_in = jnp.where(lane_id < cells_y + STEPS, after, 0)
    lane_in = jnp.where(lane_id >= lanes - STEPS, before, lane_in)
    lane_in = jnp.where(lane_id < cells_y, 1, lane_in)
    dt_ref[...] = jnp.where(row_in * lane_in > 0, jnp.float32(time_step), jnp.float32(0.0))

    sub = lax.broadcasted_iota(jnp.int32, (8, cells_y), 0)
    col = lax.broadcasted_iota(jnp.int32, (8, cells_y), 1)
    tiles = rows // 8

    def advance(src, dst, last):
        wide = 1 if last else 2
        inner = cells_x // 8 if last else tiles

        def body(z, carry):
            def at(t, w):
                return slice(8 * t, 8 * t + 8), slice(cells_y * w, cells_y * (w + 1))

            def load(ref, i, t, w):
                r, c = at(t, w)
                return ref[i, r, c]

            u = [[load(src, z + 1, t, w) for w in range(2)] for t in range(tiles)]

            def face_x(t, w):
                here, there = u[t][w], u[(t + 1) % tiles][w]
                turned = jnp.where(
                    sub == 7, pltpu.roll(there, 7, 0), pltpu.roll(here, 7, 0)
                )
                return load(cx, z, t, w) * (turned - here)

            def face_y(t, w):
                here, there = u[t][w], u[t][1 - w]
                turned = jnp.where(
                    col == cells_y - 1,
                    pltpu.roll(there, cells_y - 1, 1),
                    pltpu.roll(here, cells_y - 1, 1),
                )
                return load(cy, z, t, w) * (turned - here)

            before = [pltpu.roll(face_x(tiles - 1, w), 1, 0) for w in range(wide)]
            for t in range(inner):
                ys = [face_y(t, w) for w in range(2)]
                turned_y = [pltpu.roll(y, 1, 1) for y in ys]
                for w in range(wide):
                    here = u[t][w]
                    flux = load(cz, z + 1, t, w) * (load(src, z + 2, t, w) - here)
                    flux = flux + load(cz, z, t, w) * (load(src, z, t, w) - here)
                    side = face_x(t, w)
                    flux = flux + side
                    turned = pltpu.roll(side, 1, 0)
                    flux = flux - jnp.where(sub == 0, before[w], turned)
                    before[w] = turned
                    flux = flux + ys[w]
                    flux = flux - jnp.where(col == 0, turned_y[1 - w], turned_y[w])
                    r, c = at(t, w)
                    loss = flux - load(rr, z, t, w) * here
                    if last:
                        out_ref[z, r, c] = here + time_step * loss
                    elif w == 0 and t < cells_x // 8:
                        dst[z + 1, r, c] = here + time_step * loss
                    else:
                        dst[z + 1, r, c] = here + dt_ref[r, c] * loss
            return carry

        lax.fori_loop(0, depth, body, 0)

    src, dst = ua, ub
    for step in range(STEPS):
        advance(src, dst, step == STEPS - 1)
        src, dst = dst, src
    table_rows(lambda z: u_ref[z], table_ref, 0, depth)
    table_rows(lambda z: out_ref[z], table_ref, 1, depth)


def solve(field, conductivity, rate):
    depth, cells_x, cells_y = field.shape
    rows, lanes = cells_x + 2 * STEPS, 2 * cells_y
    arrays = (field, conductivity, rate)
    first = jnp.stack([x[:, :STEPS] for x in arrays])
    last = jnp.stack([x[:, cells_x - STEPS :] for x in arrays])
    below, above = exchange(first, last, "gx")
    halo = jnp.concatenate([below, above], 2)
    first, last = pack_sides(*arrays, halo)
    right, left = exchange(first, last, "gy")
    pos = [lax.axis_index("gx"), lax.axis_index("gy"), lax.axis_size("gx"), lax.axis_size("gy")]
    pos = jnp.stack([jnp.asarray(p, jnp.int32) for p in pos])
    padded = pltpu.VMEM((depth + 2, rows, lanes), jnp.float32)
    whole = pltpu.VMEM((depth, rows, lanes), jnp.float32)
    cells = cells_x * cells_y // PW
    return pl.pallas_call(
        solve_kernel,
        out_shape=(
            jax.ShapeDtypeStruct(field.shape, jnp.float32),
            jax.ShapeDtypeStruct((cells, 2 * depth * PW), jnp.bfloat16),
        ),
        in_specs=[pl.BlockSpec(memory_space=pltpu.SMEM)]
        + [pl.BlockSpec(memory_space=pltpu.VMEM)] * 6,
        out_specs=(pl.BlockSpec(memory_space=pltpu.VMEM),) * 2,
        scratch_shapes=[padded, padded, padded, whole, whole, whole,
            pltpu.VMEM((depth + 1, rows, lanes), jnp.float32),
            pltpu.VMEM((rows, lanes), jnp.float32)],
        cost_estimate=pl.CostEstimate(
            flops=40 * STEPS * depth * rows * lanes, bytes_accessed=64 << 20, transcendentals=0
        ),
        name="solve",
    )(pos, *arrays, halo, right, left)


def adam(param, moment, second, grad):
    moment_new = beta_one * moment + (1.0 - beta_one) * grad
    second_new = beta_two * second + (1.0 - beta_two) * grad * grad
    mhat = moment_new / (1.0 - beta_one**adam_count)
    vhat = second_new / (1.0 - beta_two**adam_count)
    return (param - learn_rate * mhat / (jnp.sqrt(vhat) + tiny_eps), moment_new, second_new)


def chip_groups(devices):
    return [list(range(core, devices, 2)) for core in range(2)]


def swap_cores(x, devices):
    return lax.ppermute(x, AXES, [(d, d ^ 1) for d in range(devices)])


def chips_all_to_all(x, devices):
    return lax.all_to_all(
        x, AXES, 0, 0, tiled=True, axis_index_groups=chip_groups(devices)
    )


def gather_params(weights, biases, hist, core, devices):
    chips = devices // 2
    layers, own, width = weights.shape
    extra = jnp.zeros((layers, own, devices), jnp.bfloat16)
    extra = extra.at[0, 0, :].set(hist.astype(jnp.bfloat16))
    extra = extra.at[:, 1, :own].set(biases.astype(jnp.bfloat16))
    pay = jnp.concatenate([weights.astype(jnp.bfloat16), extra], -1)
    got = chips_all_to_all(jnp.broadcast_to(pay[None], (chips,) + pay.shape), devices)
    other = swap_cores(got, devices)
    first = jnp.where(core == 0, got, other)
    second = jnp.where(core == 0, other, got)
    both = jnp.stack([first, second], 1).transpose(2, 0, 1, 3, 4)
    full = both.reshape(layers, devices * own, width + devices)
    tail = full[:, :, width:].reshape(layers, devices, own, devices)
    counts = jnp.sum(tail[0, :, 0, :].astype(jnp.float32), 0)
    bfull = tail[:, :, 1, :own].reshape(layers, devices * own).astype(jnp.float32)
    return full[:, :, :width], bfull, counts


def chunks(grad, devices):
    rows, width = grad.shape
    own = rows // devices
    tiles = width // 128
    grad = grad.reshape(devices // 2, 2, own, tiles, 128)
    return grad.transpose(1, 0, 3, 2, 4).reshape(2, devices // 2, tiles * own, 128)


def unchunk(share, own, width):
    return share.reshape(width // 128, own, 128).transpose(1, 0, 2).reshape(own, width)


def reduce_chunks(parts, core, devices):
    mine = lax.dynamic_index_in_dim(parts, core, 0, keepdims=False)
    theirs = lax.dynamic_index_in_dim(parts, 1 - core, 0, keepdims=False)
    theirs = swap_cores(theirs, devices)
    mine = mine + theirs
    return jnp.sum(chips_all_to_all(mine, devices), 0)


def step_all(
    field,
    conductivity,
    rate,
    patch_cell,
    trainer,
    res_slot,
    reservoir,
    weights,
    w_mom,
    w_var,
    biases,
    b_mom,
    b_var,
):
    _, cells_x, cells_y = field.shape
    devices = lax.axis_size("gx") * lax.axis_size("gy")
    me = lax.axis_index(AXES)
    core = me & 1
    own, width = weights.shape[1:]
    ids = jnp.arange(devices, dtype=jnp.int32)
    onehot = trainer == ids[None, :]
    hist = jnp.sum(onehot.astype(jnp.float32), 0)
    wfull, bfull, counts = gather_params(weights, biases, hist, core, devices)

    state, table = solve(field, conductivity, rate)
    blocks = cells_y // PW
    place = patch_cell % blocks * cells_x + patch_cell // blocks
    pick = place[:, None] == jnp.arange(table.shape[0], dtype=jnp.int32)[None, :]
    patches = jnp.dot(pick.astype(jnp.bfloat16), table, preferred_element_type=jnp.float32)
    patches = patches.astype(jnp.bfloat16)

    old = res_slot.shape[0]
    sizes = old + counts
    own_size = jnp.sum(jnp.where(ids == me, sizes, 0.0))
    new_size = jnp.sum(jnp.where(onehot, sizes[None, :], 0.0), 1)
    sizes_of = jnp.concatenate([jnp.broadcast_to(own_size, (old,)), new_size])[:, None]
    stored = reservoir[res_slot]
    rows = jnp.concatenate([stored, patches], 0)

    inputs = rows[:, :width]
    target = rows[:, width:].astype(jnp.float32)
    pre = jnp.dot(inputs, wfull[0], preferred_element_type=jnp.float32) + bfull[0]
    hidden = jnp.tanh(pre)
    hidden_b = hidden.astype(jnp.bfloat16)
    pred = jnp.dot(hidden_b, wfull[1], preferred_element_type=jnp.float32) + bfull[1]
    grad_pred = 2.0 * (pred - target) / sizes_of
    grad_pred_b = grad_pred.astype(jnp.bfloat16)
    grad_w2 = jnp.dot(hidden_b.T, grad_pred_b, preferred_element_type=jnp.float32)
    share_w2 = reduce_chunks(chunks(grad_w2, devices), core, devices)
    grad_hid = jnp.dot(grad_pred_b, wfull[1].T, preferred_element_type=jnp.float32)
    grad_pre = grad_hid * (1.0 - hidden * hidden)
    grad_pre_b = grad_pre.astype(jnp.bfloat16)
    grad_b0 = jnp.sum(grad_pre, 0)
    grad_w1 = jnp.dot(inputs.T, grad_pre_b, preferred_element_type=jnp.float32)
    grad_b = jnp.stack([grad_b0, jnp.sum(grad_pred, 0)])
    tile_b = grad_b.reshape(2, devices // 2, 2, own).transpose(2, 1, 0, 3)
    tile_b = jnp.pad(tile_b, ((0, 0), (0, 0), (0, 8 - 2), (0, 128 - own)))
    parts = jnp.concatenate([chunks(grad_w1, devices), tile_b], 2)
    share_w1 = reduce_chunks(parts, core, devices)
    share_w = jnp.stack(
        [unchunk(share_w1[: own * width // 128], own, width), unchunk(share_w2, own, width)]
    )
    share_b = share_w1[own * width // 128 :][:2, :own]
    new_w, new_wm, new_wv = adam(weights, w_mom, w_var, share_w)
    new_b, new_bm, new_bv = adam(biases, b_mom, b_var, share_b)
    return (state, new_w, new_wm, new_wv, new_b, new_bm, new_bv)


def solution(mesh):
    return jax.shard_map(
        step_all,
        mesh=mesh,
        in_specs=(
            P(None, "gx", "gy"),
            P(None, "gx", "gy"),
            P(None, "gx", "gy"),
            P(("gx", "gy")),
            P(("gx", "gy"), None),
            P(("gx", "gy")),
            P(("gx", "gy"), None),
            P(None, ("gx", "gy"), None),
            P(None, ("gx", "gy"), None),
            P(None, ("gx", "gy"), None),
            P(None, ("gx", "gy")),
            P(None, ("gx", "gy")),
            P(None, ("gx", "gy")),
        ),
        out_specs=(
            P(None, "gx", "gy"),
            P(None, ("gx", "gy"), None),
            P(None, ("gx", "gy"), None),
            P(None, ("gx", "gy"), None),
            P(None, ("gx", "gy")),
            P(None, ("gx", "gy")),
            P(None, ("gx", "gy")),
        ),
        check_vma=False,
    )
```

profile of v0, /device:TPU:0, one launch (start us, length us, event | category | flops | bytes accessed | tf_op | source)
XLA Modules:
  0.0 236.9 jit_solution(323341168139047760)
XLA Ops:
  3.3 44.3 %all_to_all.15 = bf16[64,2,8,1152]{3,2,1,0:T(8,128)(2,1)S(1)} all-to-all(bf16[64,2,8,1152]{3,2,1,0:T(8,128)(2,1)S(1)} %broadcast_in_dim.21), channel_id=1, replica_groups={{0,2,4,6,8,10,12,14,16,18,20,22,24,26,28,30,32,34,36,38,40,42,44,46,48,..., dimensions={0} | all-to-all | bytes 4718592 | tf_op jit(solution)/shard_map/all_to_all | solution.py:262
  47.7 1.6 copy.36
  49.3 1.0 slice_bitcast_fusion.11
  50.3 1.2 slice_bitcast_fusion.9
  51.5 1.3 collective-permute-start
  52.9 4.6 %collective-permute-start.1 = (f32[3,32,4,128]{3,2,1,0:T(4,128)S(1)}, f32[3,32,4,128]{3,2,1,0:T(4,128)S(1)}, u32[]{:S(2)}, u32[]{:S(2)}) collective-permute-start(f32[3,32,4,128]{3,2,1,0:T(4,128)S(1)} %pad_maximum_fusion.4), channel_id=1, source_target_pairs={{0,8},{8,16},{16,24},{24,32},{32,40},{40,48},{48,56},{56,64},{64,7... | collective-permute-start | bytes 589832 | tf_op jit(solution)/shard_map/ppermute | solution.py:29
  57.5 13.3 %gather_fusion = bf16[1024,2048]{1,0:T(8,128)(2,1)} fusion(bf16[2048,2048]{1,0:T(8,128)(2,1)} %param.23, s32[1024]{0:T(1024)S(1)} %fusion.13), kind=kCustom, calls=%fused_computation | custom fusion | bytes 8392704 | tf_op jit(solution)/shard_map/gather | solution.py:343
  71.7 3.8 %pack_sides.1 = (f32[3,72,128]{2,1,0:T(8,128)}, f32[3,72,128]{2,1,0:T(8,128)}) custom-call(f32[32,64,128]{2,1,0:T(8,128)} %u_ref.3, f32[32,64,128]{2,1,0:T(8,128)} %k_ref.3, f32[32,64,128]{2,1,0:T(8,128)} %r_ref.3, f32[3,32,8,128]{3,2,1,0:T(8,128)} %pad_maximum_fusion.2.halo_ref), custom_call_target="tpu_custom_call" | custom-call | flops 16777216 | bytes 12582912 | tf_op jit(solution)/shard_map/pack_sides/pallas_call | solution.py:56
  75.4 1.3 collective-permute-start.2
  76.7 3.2 %collective-permute-start.3 = (f32[3,72,128]{2,1,0:T(8,128)}, f32[3,72,128]{2,1,0:T(8,128)S(1)}, u32[]{:S(2)}, u32[]{:S(2)}) collective-permute-start(f32[3,72,128]{2,1,0:T(8,128)} %get-tuple-element.36), channel_id=1, source_target_pairs={{0,1},{1,2},{2,3},{3,4},{4,5},{5,6},{6,7},{8,9},{9,10},{10,11},{11... | collective-permute-start | bytes 331784 | tf_op jit(solution)/shard_map/ppermute | solution.py:29
  81.8 31.2 %solve.1 = (f32[32,64,128]{2,1,0:T(8,128)}, bf16[256,2048]{1,0:T(8,128)(2,1)}) custom-call(s32[4]{0:T(128)} %pad_add_fusion.pos_ref, f32[32,64,128]{2,1,0:T(8,128)} %u_ref.3, f32[32,64,128]{2,1,0:T(8,128)} %k_ref.3, f32[32,64,128]{2,1,0:T(8,128)} %r_ref.3, f32[3,32,8,128]{3,2,1,0:T(8,128)} %pad_maximum_fusion.2.halo_ref, f32[3,72,128]{2,1,0:T(8,128)} %copy-done.7, ...), custom_call_target="tpu_custom_call" | custom-call | flops 94371840 | bytes 67108864 | tf_op jit(solution)/shard_map/solve/pallas_call | solution.py:226
  113.0 1.7 convolution_convert_fusion
  114.8 2.5 %select_bitcast_fusion.1 = (bf16[64,1,2,8,1152]{4,3,1,0,2:T(8,128)(2,1)S(1)}, bf16[64,1,2,8,1152]{4,3,1,0,2:T(8,128)(2,1)S(1)}) fusion(bf16[64,2,8,1152]{3,2,0,1:T(8,128)(2,1)} %collective-permute-done.4, pred[]{:T(512)S(6)} %eq.43, bf16[64,2,8,1152]{3,2,1,0:T(8,128)(2,1)S(1)} %all_to_all.15), kind=kLoop, calls=%fused_computation.18 | loop fusion | flops 2359296 | bytes 9437185 | tf_op jit(solution)/shard_map/stack | solution.py:278
  117.7 2.1 copy-done.2
  121.2 5.3 %fusion.4 = f32[1280,1024]{1,0:T(8,128)S(1)} fusion(bf16[2,1024,1152]{2,1,0:T(8,128)(2,1)} %bitcast.86, bf16[1024,2048]{1,0:T(8,128)(2,1)} %gather_fusion, bf16[256,2048]{1,0:T(8,128)(2,1)S(1)} %convolution_convert_fusion), kind=kOutput, calls=%fused_computation.21 | convolution fusion | flops 2689597440 | bytes 12582912 | tf_op jit(solution)/shard_map/dot_general | solution.py:348
  127.2 4.3 %fusion.23 = (f32[1024]{0:T(1024)S(1)}, bf16[1280,1024]{1,0:T(8,128)(2,1)S(1)}) fusion(f32[1280]{0:T(1024)S(1)} %concatenate.24, bf16[256,2048]{1,0:T(8,128)(2,1)S(1)} %convolution_convert_fusion, bf16[1024,2048]{1,0:T(8,128)(2,1)S(1)} %copy-done.3, f32[1024]{0:T(1024)S(1)} %add.105, bf16[2,1024,1152]{2,1,0:T(8,128)(2,1)S(1)} %bitcast.89, ...), kind=kOutput, calls=%fused_computation.73 | convolution fusion | flops 2700082176 | bytes 15224832 | tf_op jit(solution)/shard_map/dot_general | solution.py:351
  131.6 3.0 %fusion.5 = f32[1024,1024]{1,0:T(8,128)S(1)} fusion(bf16[1280,1024]{1,0:T(8,128)(2,1)S(1)} %get-tuple-element.58, f32[1280,1024]{1,0:T(8,128)S(1)} %fusion.4, f32[1024]{0:T(1024)S(1)} %add.102), kind=kOutput, calls=%fused_computation.24 | convolution fusion | flops 2686976000 | bytes 12062720 | tf_op jit(solution)/shard_map/dot_general | solution.py:354
  134.6 2.0 copy-done.4
  136.6 1.5 dynamic-slice_bitcast_fusion.1
  138.1 1.8 collective-permute-start.6
  139.9 4.9 %fusion.24 = (f32[1024]{0:T(1024)S(1)}, bf16[1280,1024]{1,0:T(8,128)(2,1)}) fusion(f32[1280,1024]{1,0:T(8,128)S(1)} %fusion.4, f32[1024]{0:T(1024)S(1)} %add.102, bf16[2,1024,1152]{2,1,0:T(8,128)(2,1)S(1)} %bitcast.90, bf16[1280,1024]{1,0:T(8,128)(2,1)S(1)} %get-tuple-element.58), kind=kOutput, calls=%fused_computation.74 | convolution fusion | flops 2692217856 | bytes 12591104 | tf_op jit(solution)/shard_map/dot_general | solution.py:356
  145.5 5.3 %fusion.2 = f32[1024,1024]{1,0:T(8,128)S(1)} fusion(bf16[1280,1024]{1,0:T(8,128)(2,1)} %get-tuple-element.60, bf16[1024,2048]{1,0:T(8,128)(2,1)} %gather_fusion, bf16[256,2048]{1,0:T(8,128)(2,1)} %copy-done.5), kind=kOutput, calls=%fused_computation.12 | convolution fusion | flops 2689597440 | bytes 12058624 | tf_op jit(solution)/shard_map/dot_general | solution.py:360
  151.3 2.1 copy-done
  153.4 1.5 dynamic-slice_bitcast_fusion
  154.9 3.3 %bitcast_add_fusion.1 = f32[64,64,128]{2,1,0:T(8,128)} fusion(f32[64,64,128]{2,1,0:T(8,128)S(1)} %collective-permute-done.6, f32[2,64,64,128]{3,2,0,1:T(8,128)} %bitcast.92, s32[]{:T(128)S(6)} %select_n.53), kind=kLoop, calls=%fused_computation.22 | loop fusion | flops 524288 | bytes 6291460 | tf_op jit(solution)/shard_map/add | solution.py:302
  158.2 8.9 %all-to-all-start.2 = ((f32[64,64,128]{2,1,0:T(8,128)}), f32[64,64,128]{2,1,0:T(8,128)S(1)}, u32[]{:S(2)}, u32[]{:S(2)}) async-start(f32[64,64,128]{2,1,0:T(8,128)} %bitcast_add_fusion.1), calls=%async_computation.2 | async-start | bytes 4194304 | tf_op jit(solution)/shard_map/all_to_all | solution.py:262
  167.1 4.1 %bitcast_add_fusion = f32[64,72,128]{2,1,0:T(8,128)} fusion(f32[64,72,128]{2,1,0:T(8,128)} %collective-permute-done.5, f32[2,64,72,128]{3,2,0,1:T(8,128)} %copy-done, s32[]{:T(128)S(6)} %select_n.53), kind=kLoop, calls=%fused_computation.15 | loop fusion | flops 589824 | bytes 7077892 | tf_op jit(solution)/shard_map/add | solution.py:302
  171.3 25.6 %all-to-all-done.2 = f32[64,64,128]{2,1,0:T(8,128)S(1)} async-done(((f32[64,64,128]{2,1,0:T(8,128)}), f32[64,64,128]{2,1,0:T(8,128)S(1)}, u32[]{:S(2)}, u32[]{:S(2)}) %all-to-all-start.2) | async-done | bytes 2097184 | tf_op jit(solution)/shard_map/all_to_all | solution.py:262
  196.9 1.3 copy-done.1
  198.2 6.3 %all-to-all-start.1 = ((f32[64,72,128]{2,1,0:T(8,128)}), f32[64,72,128]{2,1,0:T(8,128)S(1)}, u32[]{:S(2)}, u32[]{:S(2)}) async-start(f32[64,72,128]{2,1,0:T(8,128)} %bitcast_add_fusion), calls=%async_computation.1 | async-start | bytes 4718592 | tf_op jit(solution)/shard_map/all_to_all | solution.py:262
  204.5 1.7 reduce_sum.79
  206.3 29.2 %all-to-all-done.1 = f32[64,72,128]{2,1,0:T(8,128)S(1)} async-done(((f32[64,72,128]{2,1,0:T(8,128)}), f32[64,72,128]{2,1,0:T(8,128)S(1)}, u32[]{:S(2)}, u32[]{:S(2)}) %all-to-all-start.1) | async-done | bytes 2359328 | tf_op jit(solution)/shard_map/all_to_all | solution.py:262
  (80 shorter events, 10.5 us)
Async XLA Ops:
  47.7 9.8 %copy-start.11 = (s32[1024]{0:T(1024)S(1)}, s32[1024]{0:T(1024)}, u32[]{:S(2)}) copy-start(s32[1024]{0:T(1024)} %param.22) | copy-start | bytes 12292
  49.3 65.5 %collective-permute-start.4 = (bf16[64,2,8,1152]{3,2,0,1:T(8,128)(2,1)}, bf16[64,2,8,1152]{3,2,0,1:T(8,128)(2,1)}, u32[]{:S(2)}, u32[]{:S(2)}) collective-permute-start(bf16[64,2,8,1152]{3,2,0,1:T(8,128)(2,1)} %copy.36), channel_id=1, source_target_pairs={{0,1},{1,0},{2,3},{3,2},{4,5},{5,4},{6,7},{7,6},{8,9},{9,8},{10,11... | collective-permute-start | bytes 7077896 | tf_op jit(solution)/shard_map/ppermute | solution.py:258
  51.5 19.3 %collective-permute-start = (f32[3,32,4,128]{3,2,1,0:T(4,128)S(1)}, f32[3,32,4,128]{3,2,1,0:T(4,128)S(1)}, u32[]{:S(2)}, u32[]{:S(2)}) collective-permute-start(f32[3,32,4,128]{3,2,1,0:T(4,128)S(1)} %pad_maximum_fusion.3), channel_id=1, source_target_pairs={{8,0},{16,8},{24,16},{32,24},{40,32},{48,40},{56,48},{64,56},{72,6... | collective-permute-start | bytes 589832 | tf_op jit(solution)/shard_map/ppermute | solution.py:29
  52.9 18.0 %collective-permute-start.1 = (f32[3,32,4,128]{3,2,1,0:T(4,128)S(1)}, f32[3,32,4,128]{3,2,1,0:T(4,128)S(1)}, u32[]{:S(2)}, u32[]{:S(2)}) collective-permute-start(f32[3,32,4,128]{3,2,1,0:T(4,128)S(1)} %pad_maximum_fusion.4), channel_id=1, source_target_pairs={{0,8},{8,16},{16,24},{24,32},{32,40},{40,48},{48,56},{56,64},{64,7... | collective-permute-start | bytes 589832 | tf_op jit(solution)/shard_map/ppermute | solution.py:29
  57.5 13.3 %copy-start.15 = (s32[256]{0:T(256)S(1)}, s32[256]{0:T(256)}, u32[]{:S(2)}) copy-start(s32[256]{0:T(256)} %param.20) | copy-start | bytes 3076
  75.4 5.1 %collective-permute-start.2 = (f32[3,72,128]{2,1,0:T(8,128)}, f32[3,72,128]{2,1,0:T(8,128)S(1)}, u32[]{:S(2)}, u32[]{:S(2)}) collective-permute-start(f32[3,72,128]{2,1,0:T(8,128)} %get-tuple-element.35), channel_id=1, source_target_pairs={{1,0},{2,1},{3,2},{4,3},{5,4},{6,5},{7,6},{9,8},{10,9},{11,10},{12... | collective-permute-start | bytes 331784 | tf_op jit(solution)/shard_map/ppermute | solution.py:29
  76.7 4.2 %collective-permute-start.3 = (f32[3,72,128]{2,1,0:T(8,128)}, f32[3,72,128]{2,1,0:T(8,128)S(1)}, u32[]{:S(2)}, u32[]{:S(2)}) collective-permute-start(f32[3,72,128]{2,1,0:T(8,128)} %get-tuple-element.36), channel_id=1, source_target_pairs={{0,1},{1,2},{2,3},{3,4},{4,5},{5,6},{6,7},{8,9},{9,10},{10,11},{11... | collective-permute-start | bytes 331784 | tf_op jit(solution)/shard_map/ppermute | solution.py:29
  80.5 0.7 copy-start.7
  81.2 0.6 copy-start.8
  114.7 12.4 %copy-start.5 = (bf16[256,2048]{1,0:T(8,128)(2,1)}, bf16[256,2048]{1,0:T(8,128)(2,1)S(1)}, u32[]{:S(2)}) copy-start(bf16[256,2048]{1,0:T(8,128)(2,1)S(1)} %convolution_convert_fusion) | copy-start | bytes 3145732
  117.2 3.6 %copy-start.16 = (s32[256,1]{0,1:T(1,128)S(1)}, s32[256,1]{0,1:T(1,128)}, u32[]{:S(2)}) copy-start(s32[256,1]{0,1:T(1,128)} %param.21) | copy-start | bytes 3076
  117.7 2.1 copy-start.2
  121.0 6.2 %slice-start = ((s8[4718592]{0:T(1024)(128)(4,1)}), s8[524288]{0:T(1024)(128)(4,1)S(1)}, s32[]{:S(2)}) async-start(s8[4718592]{0:T(1024)(128)(4,1)} %bitcast.87), calls=%async_computation.3 | async-start | bytes 1048576
  121.2 6.0 %slice-start.1 = ((s8[4718592]{0:T(1024)(128)(4,1)}), s8[4194304]{0:T(1024)(128)(4,1)S(1)}, s32[]{:S(2)}) async-start(s8[4718592]{0:T(1024)(128)(4,1)} %bitcast.87), calls=%async_computation.4 | async-start | bytes 8388608
  121.2 6.0 %copy-start.3 = (bf16[1024,2048]{1,0:T(8,128)(2,1)S(1)}, bf16[1024,2048]{1,0:T(8,128)(2,1)}, u32[]{:S(2)}) copy-start(bf16[1024,2048]{1,0:T(8,128)(2,1)} %gather_fusion) | copy-start | bytes 12582916
  134.5 2.1 copy-start.4
  138.1 16.8 %collective-permute-start.6 = (f32[64,64,128]{2,1,0:T(8,128)}, f32[64,64,128]{2,1,0:T(8,128)S(1)}, u32[]{:S(2)}, u32[]{:S(2)}) collective-permute-start(f32[64,64,128]{2,1,0:T(8,128)} %dynamic-slice_bitcast_fusion.1), channel_id=1, source_target_pairs={{0,1},{1,0},{2,3},{3,2},{4,5},{5,4},{6,7},{7,6},{8,9},{9,8},{10,11... | collective-permute-start | bytes 6291464 | tf_op jit(solution)/shard_map/ppermute | solution.py:258
  151.2 2.1 copy-start
  154.9 12.2 %collective-permute-start.5 = (f32[64,72,128]{2,1,0:T(8,128)}, f32[64,72,128]{2,1,0:T(8,128)}, u32[]{:S(2)}, u32[]{:S(2)}) collective-permute-start(f32[64,72,128]{2,1,0:T(8,128)} %dynamic-slice_bitcast_fusion), channel_id=1, source_target_pairs={{0,1},{1,0},{2,3},{3,2},{4,5},{5,4},{6,7},{7,6},{8,9},{9,8},{10,11... | collective-permute-start | bytes 7077896 | tf_op jit(solution)/shard_map/ppermute | solution.py:258
  158.2 38.7 %all-to-all-start.2 = ((f32[64,64,128]{2,1,0:T(8,128)}), f32[64,64,128]{2,1,0:T(8,128)S(1)}, u32[]{:S(2)}, u32[]{:S(2)}) async-start(f32[64,64,128]{2,1,0:T(8,128)} %bitcast_add_fusion.1), calls=%async_computation.2 | async-start | bytes 4194304 | tf_op jit(solution)/shard_map/all_to_all | solution.py:262
  171.2 64.4 %copy-start.12 = (f32[2,8]{1,0:T(2,128)S(1)}, f32[2,8]{1,0:T(2,128)}, u32[]{:S(2)}) copy-start(f32[2,8]{1,0:T(2,128)} %param.27) | copy-start | bytes 196
  171.2 64.4 %copy-start.13 = (f32[2,8]{1,0:T(2,128)S(1)}, f32[2,8]{1,0:T(2,128)}, u32[]{:S(2)}) copy-start(f32[2,8]{1,0:T(2,128)} %param.28) | copy-start | bytes 196
  171.2 64.4 %copy-start.14 = (f32[2,8]{1,0:T(2,128)S(1)}, f32[2,8]{1,0:T(2,128)}, u32[]{:S(2)}) copy-start(f32[2,8]{1,0:T(2,128)} %param.29) | copy-start | bytes 196
  171.2 65.0 %copy-start.6 = (f32[2,8,1024]{2,1,0:T(8,128)S(1)}, f32[2,8,1024]{2,1,0:T(8,128)}, u32[]{:S(2)}) copy-start(f32[2,8,1024]{2,1,0:T(8,128)} %param.24) | copy-start | bytes 196612
  171.3 65.0 %copy-start.9 = (f32[2,8,1024]{2,1,0:T(8,128)S(1)}, f32[2,8,1024]{2,1,0:T(8,128)}, u32[]{:S(2)}) copy-start(f32[2,8,1024]{2,1,0:T(8,128)} %param.25) | copy-start | bytes 196612
  171.3 65.0 %copy-start.10 = (f32[2,8,1024]{2,1,0:T(8,128)S(1)}, f32[2,8,1024]{2,1,0:T(8,128)}, u32[]{:S(2)}) copy-start(f32[2,8,1024]{2,1,0:T(8,128)} %param.26) | copy-start | bytes 196612
  196.9 1.3 copy-start.1
  198.2 37.2 %all-to-all-start.1 = ((f32[64,72,128]{2,1,0:T(8,128)}), f32[64,72,128]{2,1,0:T(8,128)S(1)}, u32[]{:S(2)}, u32[]{:S(2)}) async-start(f32[64,72,128]{2,1,0:T(8,128)} %bitcast_add_fusion), calls=%async_computation.1 | async-start | bytes 4718592 | tf_op jit(solution)/shard_map/all_to_all | solution.py:262
where the time goes:
time: 238 us; the launch traced here: 237 us
  waiting for transfers between devices  55.2 us (23%)
  blocking collectives  44.3 us (19%)
  Pallas kernels  35 us (15%)
  local copies, waits for them, and re-layouts  30.7 us (13%)
  starting transfers between devices  27.4 us (12%)
  matrix products  24.5 us (10%)
  other arithmetic  18.8 us (8%)
    all_to_all x2, waiting for transfers between devices, chips_all_to_all(): lax.all_to_all(x, AXES, 0, 0, tiled=True, axis_index_groups=chip_groups(d...  54.8 us
    all_to_all x1, blocking collectives, chips_all_to_all(): lax.all_to_all(x, AXES, 0, 0, tiled=True, axis_index_groups=chip_groups(d...  44.3 us
    pallas_call x1, Pallas kernels, solve(): pl.pallas_call(solve_kernel, out_shape=(jax.ShapeDtypeStruct(field.shape,...  31.2 us
    all_to_all x2, starting transfers between devices, chips_all_to_all(): lax.all_to_all(x, AXES, 0, 0, tiled=True, axis_index_groups=chip_groups(d...  15.2 us
    gather x1, local copies, waits for them, and re-layouts, step_all(): stored = reservoir[res_slot]  13.3 us
    ppermute x4, starting transfers between devices, exchange(): return (lax.ppermute(first, axis, down), lax.ppermute(last, axis, up))  10.3 us
    unnamed x39, local copies, waits for them, and re-layouts  8.75 us
    add x2, other arithmetic, reduce_chunks(): mine = mine + theirs  7.38 us
  transfers between devices with their start and end apart: 9, of which 3 were waited for; matrix products, arithmetic and copies ran while one was open for 17% of the time, Pallas kernels for 15%

commit v1 on v0

--- a/solution.py
+++ b/solution.py
@@ -76,6 +76,9 @@
         return carry
 
     lax.fori_loop(0, depth // per, body, 0)
+
+
+MARGIN = 8
 
 
 def solve_kernel(
@@ -98,104 +101,117 @@
     dt_ref,
 ):
     depth, cells_x, cells_y = u_ref.shape
-    rows, lanes = cells_x + 2 * STEPS, 2 * cells_y
+    halo_top, main = MARGIN, 2 * MARGIN
+    halo_low, end = main + cells_x, main + cells_x + MARGIN
     lane = lane_ids((1, cells_y))
-    blank = jnp.zeros((rows, lanes), jnp.float32)
-    for ref in (ua, ub, kk):
-        ref[0] = blank
-        ref[depth + 1] = blank
+    sub = lax.broadcasted_iota(jnp.int32, (8, cells_y), 0)
+    col = lax.broadcasted_iota(jnp.int32, (8, cells_y), 1)
+    blank = jnp.zeros((end + MARGIN, cells_y), jnp.float32)
+    edge = jnp.zeros((MARGIN, cells_y), jnp.float32)
+    for w in range(2):
+        for ref in (ua, ub, kk):
+            ref[w, 0] = blank
+            ref[w, depth + 1] = blank
+
+    def clear(z, carry):
+        for w in range(2):
+            for ref in (ua, ub, kk):
+                ref[w, z + 1, 0:halo_top, :] = edge
+                ref[w, z + 1, end : end + MARGIN, :] = edge
+        return carry
+
+    lax.fori_loop(0, depth, clear, 0)
+
+    def place(ref, w, at, body, ends):
+        ref[w, at, main:halo_low, :] = body
+        ref[w, at, halo_top:main, :] = jnp.where(sub >= STEPS, ends, 0.0)
+        ref[w, at, halo_low:end, :] = jnp.where(sub < STEPS, ends, 0.0)
+
     for z in range(depth):
         for a, (src, dst, at) in enumerate(((u_ref, ua, z + 1), (k_ref, kk, z + 1), (r_ref, rr, z))):
-            dst[at, 0:cells_x, 0:cells_y] = src[z]
-            dst[at, cells_x:rows, 0:cells_y] = halo_ref[a, z]
+            place(dst, 0, at, src[z], halo_ref[a, z])
             turn = -z * STEPS % cells_y
-            right, left = right_ref[a], left_ref[a]
+            side = jnp.where(lane // STEPS == z, right_ref[a], left_ref[a])
             if turn:
-                right, left = pltpu.roll(right, turn, 1), pltpu.roll(left, turn, 1)
-            side = jnp.where(lane < STEPS, right, 0.0)
-            side = jnp.where(lane >= cells_y - STEPS, left, side)
-            dst[at, :, cells_y:lanes] = side
+                side = pltpu.roll(side, turn, 1)
+            place(dst, 1, at, side[:cells_x], side[cells_x:])
+
+    def rows(t, shift=0):
+        return slice(8 * t + shift, 8 * t + 8 + shift)
+
+    def turned(pair, back):
+        amount = 1 if back else cells_y - 1
+        seam = col == (0 if back else cells_y - 1)
+        both = [pltpu.roll(x, amount, 1) for x in pair]
+        return [jnp.where(seam, both[1 - w], both[w]) for w in range(2)]
+
+    tiles = end // 8
+    half = 0.5 * time_step
 
     def faces(z, carry):
-        k = kk[z + 1]
-        cz[z] = 0.5 * (kk[z] + k)
-        cx[z] = 0.5 * (k + pltpu.roll(k, rows - 1, 0))
-        cy[z] = 0.5 * (k + pltpu.roll(k, lanes - 1, 1))
+        for t in range(tiles):
+            k = [kk[w, z + 1, rows(t), :] for w in range(2)]
+            after = turned(k, False)
+            for w in range(2):
+                cz[w, z, rows(t), :] = half * (kk[w, z, rows(t), :] + k[w])
+                cx[w, z, rows(t), :] = half * (k[w] + kk[w, z + 1, rows(t, 1), :])
+                cy[w, z, rows(t), :] = half * (k[w] + after[w])
         return carry
 
     lax.fori_loop(0, depth, faces, 0)
-    cz[depth] = 0.5 * kk[depth]
+    for w in range(2):
+        cz[w, depth] = half * kk[w, depth]
+
+    def keeps(z, carry):
+        for t in range(halo_top // 8, tiles):
+            ys = [cy[w, z, rows(t), :] for w in range(2)]
+            back = turned(ys, True)
+            for w in range(2):
+                loss = cz[w, z + 1, rows(t), :] + cz[w, z, rows(t), :]
+                loss = loss + (cx[w, z, rows(t), :] + cx[w, z, rows(t, -1), :])
+                loss = loss + (ys[w] + back[w])
+                rr[w, z, rows(t), :] = (1.0 - time_step * rr[w, z, rows(t), :]) - loss
+        return carry
+
+    lax.fori_loop(0, depth, keeps, 0)
 
     gx, gy = pos_ref[0], pos_ref[1]
-    row_id = lax.broadcasted_iota(jnp.int32, (rows, lanes), 0)
-    lane_id = lax.broadcasted_iota(jnp.int32, (rows, lanes), 1)
     below = jnp.where(gx < pos_ref[2] - 1, 1, 0)
     above = jnp.where(gx > 0, 1, 0)
     after = jnp.where(gy < pos_ref[3] - 1, 1, 0)
     before = jnp.where(gy > 0, 1, 0)
-    row_in = jnp.where(row_id < cells_x, 1, jnp.where(row_id < cells_x + STEPS, below, above))
-    lane_in = jnp.where(lane_id < cells_y + STEPS, after, 0)
-    lane_in = jnp.where(lane_id >= lanes - STEPS, before, lane_in)
-    lane_in = jnp.where(lane_id < cells_y, 1, lane_in)
-    dt_ref[...] = jnp.where(row_in * lane_in > 0, jnp.float32(time_step), jnp.float32(0.0))
-
-    sub = lax.broadcasted_iota(jnp.int32, (8, cells_y), 0)
-    col = lax.broadcasted_iota(jnp.int32, (8, cells_y), 1)
-    tiles = rows // 8
+    row_id = lax.broadcasted_iota(jnp.int32, blank.shape, 0)
+    lane_id = lax.broadcasted_iota(jnp.int32, blank.shape, 1)
+    row_in = jnp.where(row_id < main, above, jnp.where(row_id < halo_low, 1, below))
+    row_in = jnp.where((row_id < main - STEPS) | (row_id >= halo_low + STEPS), 0, row_in)
+    side_in = jnp.where(lane_id < STEPS, after, 0)
+    side_in = jnp.where(lane_id >= cells_y - STEPS, before, side_in)
+    for w, inside in ((0, row_in), (1, row_in * side_in)):
+        dt_ref[w] = jnp.where(inside > 0, jnp.float32(1.0), jnp.float32(0.0))
 
     def advance(src, dst, last):
-        wide = 1 if last else 2
-        inner = cells_x // 8 if last else tiles
+        picks = (0,) if last else (0, 1)
+        first_tile, end_tile = (main // 8, halo_low // 8) if last else (halo_top // 8, end // 8)
 
         def body(z, carry):
-            def at(t, w):
-                return slice(8 * t, 8 * t + 8), slice(cells_y * w, cells_y * (w + 1))
-
-            def load(ref, i, t, w):
-                r, c = at(t, w)
-                return ref[i, r, c]
-
-            u = [[load(src, z + 1, t, w) for w in range(2)] for t in range(tiles)]
-
-            def face_x(t, w):
-                here, there = u[t][w], u[(t + 1) % tiles][w]
-                turned = jnp.where(
-                    sub == 7, pltpu.roll(there, 7, 0), pltpu.roll(here, 7, 0)
-                )
-                return load(cx, z, t, w) * (turned - here)
-
-            def face_y(t, w):
-                here, there = u[t][w], u[t][1 - w]
-                turned = jnp.where(
-                    col == cells_y - 1,
-                    pltpu.roll(there, cells_y - 1, 1),
-                    pltpu.roll(here, cells_y - 1, 1),
-                )
-                return load(cy, z, t, w) * (turned - here)
-
-            before = [pltpu.roll(face_x(tiles - 1, w), 1, 0) for w in range(wide)]
-            for t in range(inner):
-                ys = [face_y(t, w) for w in range(2)]
-                turned_y = [pltpu.roll(y, 1, 1) for y in ys]
-                for w in range(wide):
-                    here = u[t][w]
-                    flux = load(cz, z + 1, t, w) * (load(src, z + 2, t, w) - here)
-                    flux = flux + load(cz, z, t, w) * (load(src, z, t, w) - here)
-                    side = face_x(t, w)
-                    flux = flux + side
-                    turned = pltpu.roll(side, 1, 0)
-                    flux = flux - jnp.where(sub == 0, before[w], turned)
-                    before[w] = turned
-                    flux = flux + ys[w]
-                    flux = flux - jnp.where(col == 0, turned_y[1 - w], turned_y[w])
-                    r, c = at(t, w)
-                    loss = flux - load(rr, z, t, w) * here
+            for t in range(first_tile, end_tile):
+                u = [src[w, z + 1, rows(t), :] for w in range(2)]
+                after = turned(u, False)
+                ys = [cy[w, z, rows(t), :] for w in range(2)]
+                back = turned([ys[w] * u[w] for w in range(2)], True)
+                for w in picks:
+                    total = cz[w, z + 1, rows(t), :] * src[w, z + 2, rows(t), :]
+                    total = total + cz[w, z, rows(t), :] * src[w, z, rows(t), :]
+                    total = total + cx[w, z, rows(t), :] * src[w, z + 1, rows(t, 1), :]
+                    total = total + cx[w, z, rows(t, -1), :] * src[w, z + 1, rows(t, -1), :]
+                    total = total + (ys[w] * after[w] + back[w])
+                    total = total + rr[w, z, rows(t), :] * u[w]
                     if last:
-                        out_ref[z, r, c] = here + time_step * loss
-                    elif w == 0 and t < cells_x // 8:
-                        dst[z + 1, r, c] = here + time_step * loss
+                        out_ref[z, rows(t - main // 8), :] = total
+                    elif w == 0 and main <= 8 * t < halo_low:
+                        dst[w, z + 1, rows(t), :] = total
                     else:
-                        dst[z + 1, r, c] = here + dt_ref[r, c] * loss
+                        dst[w, z + 1, rows(t), :] = dt_ref[w, rows(t), :] * total
             return carry
 
         lax.fori_loop(0, depth, body, 0)
@@ -210,7 +226,7 @@
 
 def solve(field, conductivity, rate):
     depth, cells_x, cells_y = field.shape
-    rows, lanes = cells_x + 2 * STEPS, 2 * cells_y
+    rows, lanes = cells_x + 4 * MARGIN, cells_y
     arrays = (field, conductivity, rate)
     first = jnp.stack([x[:, :STEPS] for x in arrays])
     last = jnp.stack([x[:, cells_x - STEPS :] for x in arrays])
@@ -220,8 +236,8 @@
     right, left = exchange(first, last, "gy")
     pos = [lax.axis_index("gx"), lax.axis_index("gy"), lax.axis_size("gx"), lax.axis_size("gy")]
     pos = jnp.stack([jnp.asarray(p, jnp.int32) for p in pos])
-    padded = pltpu.VMEM((depth + 2, rows, lanes), jnp.float32)
-    whole = pltpu.VMEM((depth, rows, lanes), jnp.float32)
+    padded = pltpu.VMEM((2, depth + 2, rows, lanes), jnp.float32)
+    whole = pltpu.VMEM((2, depth, rows, lanes), jnp.float32)
     cells = cells_x * cells_y // PW
     return pl.pallas_call(
         solve_kernel,
@@ -233,10 +249,10 @@
         + [pl.BlockSpec(memory_space=pltpu.VMEM)] * 6,
         out_specs=(pl.BlockSpec(memory_space=pltpu.VMEM),) * 2,
         scratch_shapes=[padded, padded, padded, whole, whole, whole,
-            pltpu.VMEM((depth + 1, rows, lanes), jnp.float32),
-            pltpu.VMEM((rows, lanes), jnp.float32)],
+            pltpu.VMEM((2, depth + 1, rows, lanes), jnp.float32),
+            pltpu.VMEM((2, rows, lanes), jnp.float32)],
         cost_estimate=pl.CostEstimate(
-            flops=40 * STEPS * depth * rows * lanes, bytes_accessed=64 << 20, transcendentals=0
+            flops=80 * STEPS * depth * rows * lanes, bytes_accessed=64 << 20, transcendentals=0
         ),
         name="solve",
     )(pos, *arrays, halo, right, left)
@@ -295,12 +311,47 @@
     return share.reshape(width // 128, own, 128).transpose(1, 0, 2).reshape(own, width)
 
 
-def reduce_chunks(parts, core, devices):
+def device_of(coords, core):
+    z, x, y = coords
+    return ((z * 4 + x) * 4 + y) * 2 + core
+
+
+FAR_BIT = (6, 4, 2)
+
+
+def halve(x, me, core, shifts, mask):
+    bit = jnp.where(core == 0, me >> shifts[0], me >> shifts[1]) & 1
+    keep = lax.dynamic_index_in_dim(x, bit, 0, keepdims=False)
+    send = lax.dynamic_index_in_dim(x, 1 - bit, 0, keepdims=False)
+    pairs = [(d, d ^ mask[d & 1]) for d in range(lax.axis_size(AXES))]
+    return keep + lax.ppermute(send, AXES, pairs)
+
+
+def axis_groups(axis, core):
+    four = range(4)
+    groups = []
+    for p in four:
+        places = [(q, r) for q in four for r in four]
+        coords = [tuple(pair[:axis]) + (p,) + tuple(pair[axis:]) for pair in places]
+        groups.append([device_of(c, core) for c in coords])
+    return groups
+
+
+def reduce_parts(parts, me, core, devices, axes):
     mine = lax.dynamic_index_in_dim(parts, core, 0, keepdims=False)
     theirs = lax.dynamic_index_in_dim(parts, 1 - core, 0, keepdims=False)
     theirs = swap_cores(theirs, devices)
-    mine = mine + theirs
-    return jnp.sum(chips_all_to_all(mine, devices), 0)
+    tile = parts.shape[2:]
+    mine = (mine + theirs).reshape((4, 4, 4) + tile)
+    turned = [jnp.moveaxis(mine, axis, 0) for axis in axes]
+    mine = jnp.where(core == 0, *turned).reshape((2, 2, 16) + tile)
+    far = [FAR_BIT[axis] for axis in axes]
+    near = [bit - 1 for bit in far]
+    mine = halve(mine, me, core, far, [3 << bit for bit in near])
+    mine = halve(mine, me, core, near, [1 << bit for bit in near])
+    groups = axis_groups(axes[0], 0) + axis_groups(axes[1], 1)
+    got = lax.all_to_all(mine, AXES, 0, 0, tiled=True, axis_index_groups=groups)
+    return jnp.sum(got, 0)
 
 
 def step_all(
@@ -339,20 +390,20 @@
     sizes = old + counts
     own_size = jnp.sum(jnp.where(ids == me, sizes, 0.0))
     new_size = jnp.sum(jnp.where(onehot, sizes[None, :], 0.0), 1)
-    sizes_of = jnp.concatenate([jnp.broadcast_to(own_size, (old,)), new_size])[:, None]
+    scale = 2.0 / jnp.concatenate([jnp.broadcast_to(own_size, (old,)), new_size])[:, None]
     stored = reservoir[res_slot]
     rows = jnp.concatenate([stored, patches], 0)
 
     inputs = rows[:, :width]
     target = rows[:, width:].astype(jnp.float32)
     pre = jnp.dot(inputs, wfull[0], preferred_element_type=jnp.float32) + bfull[0]
-    hidden = jnp.tanh(pre)
+    hidden = lax.optimization_barrier(jnp.tanh(pre))
     hidden_b = hidden.astype(jnp.bfloat16)
     pred = jnp.dot(hidden_b, wfull[1], preferred_element_type=jnp.float32) + bfull[1]
-    grad_pred = 2.0 * (pred - target) / sizes_of
+    grad_pred = (pred - target) * scale
     grad_pred_b = grad_pred.astype(jnp.bfloat16)
     grad_w2 = jnp.dot(hidden_b.T, grad_pred_b, preferred_element_type=jnp.float32)
-    share_w2 = reduce_chunks(chunks(grad_w2, devices), core, devices)
+    share_w2 = reduce_parts(chunks(grad_w2, devices), me, core, devices, (0, 1))
     grad_hid = jnp.dot(grad_pred_b, wfull[1].T, preferred_element_type=jnp.float32)
     grad_pre = grad_hid * (1.0 - hidden * hidden)
     grad_pre_b = grad_pre.astype(jnp.bfloat16)
@@ -362,7 +413,7 @@
     tile_b = grad_b.reshape(2, devices // 2, 2, own).transpose(2, 1, 0, 3)
     tile_b = jnp.pad(tile_b, ((0, 0), (0, 0), (0, 8 - 2), (0, 128 - own)))
     parts = jnp.concatenate([chunks(grad_w1, devices), tile_b], 2)
-    share_w1 = reduce_chunks(parts, core, devices)
+    share_w1 = reduce_parts(parts, me, core, devices, (1, 2))
     share_w = jnp.stack(
         [unchunk(share_w1[: own * width // 128], own, width), unchunk(share_w2, own, width)]
     )

time: 238 us -> 230 us (0.966); the launches traced: 237 us -> 226 us
  waiting for transfers between devices: 55.2 us -> 39.9 us
  matrix products: 24.5 us -> 30.1 us
  Pallas kernels: 35 us -> 30.7 us
    all_to_all x2, waiting for transfers between devices: 54.8 us -> 18 us  [reduce_parts(): got = lax.all_to_all(mine, AXES, 0, 0, tiled=True, axis_index_groups=groups)]
    ppermute x0 -> x4, waiting for transfers between devices: none -> 21.6 us  [halve(): return keep + lax.ppermute(send, AXES, pairs)]
    pallas_call x1, Pallas kernels: 31.2 us -> 26.9 us  [solve(): pl.pallas_call(solve_kernel, out_shape=(jax.ShapeDtypeStruct(field.shape,...]
    squeeze x2 -> x6, local copies, waits for them, and re-layouts: 3.08 us -> 6.94 us  [the longest x2 4.87 us: reduce_parts(): theirs = lax.dynamic_index_in_dim(parts, 1 - core, 0, keepdims=False)]
    ppermute x0 -> x4, starting transfers between devices: none -> 3.75 us  [halve(): return keep + lax.ppermute(send, AXES, pairs)]
    all_to_all x2, starting transfers between devices: 15.2 us -> 11.7 us  [reduce_parts(): got = lax.all_to_all(mine, AXES, 0, 0, tiled=True, axis_index_groups=groups)]
    dot_general x1, matrix products: 4.33 us -> 7.1 us  [step_all(): jnp.dot(hidden_b, wfull[1], preferred_element_type=jnp.float32) + bfull[1]]
    add x2 -> x6, other arithmetic: 7.38 us -> 8.89 us  [the longest x4 6.03 us: halve(): return keep + lax.ppermute(send, AXES, pairs)]
  transfers between devices with their start and end apart: 9 -> 13, of which waited for: 3 -> 6; matrix products, arithmetic and copies ran while one was open for 17% -> 14% of each run, Pallas kernels for 15% -> 14%
where the time goes in v1:
time: 230 us; the launch traced here: 226 us
  blocking collectives  44.3 us (19%)
  waiting for transfers between devices  39.9 us (17%)
  local copies, waits for them, and re-layouts  32.8 us (14%)
  Pallas kernels  30.7 us (13%)
  matrix products  30.1 us (13%)
  starting transfers between devices  27.6 us (12%)
  other arithmetic  19.2 us (8%)
    all_to_all x1, blocking collectives, chips_all_to_all(): lax.all_to_all(x, AXES, 0, 0, tiled=True, axis_index_groups=chip_groups(d...  44.3 us
    pallas_call x1, Pallas kernels, solve(): pl.pallas_call(solve_kernel, out_shape=(jax.ShapeDtypeStruct(field.shape,...  26.9 us
    ppermute x4, waiting for transfers between devices, halve(): return keep + lax.ppermute(send, AXES, pairs)  21.6 us
    all_to_all x2, waiting for transfers between devices, reduce_parts(): got = lax.all_to_all(mine, AXES, 0, 0, tiled=True, axis_index_groups=groups)  18 us
    gather x1, local copies, waits for them, and re-layouts, step_all(): stored = reservoir[res_slot]  13.3 us
    all_to_all x2, starting transfers between devices, reduce_parts(): got = lax.all_to_all(mine, AXES, 0, 0, tiled=True, axis_index_groups=groups)  11.7 us
    ppermute x4, starting transfers between devices, exchange(): return (lax.ppermute(first, axis, down), lax.ppermute(last, axis, up))  10.3 us
    unnamed x39, local copies, waits for them, and re-layouts  7.65 us
  transfers between devices with their start and end apart: 13, of which 6 were waited for; matrix products, arithmetic and copies ran while one was open for 14% of the time, Pallas kernels for 14%

profile of v1, /device:TPU:0, one launch (start us, length us, event | category | flops | bytes accessed | tf_op | source)
XLA Modules:
  0.0 225.8 jit_solution(13015056842457673731)
XLA Ops:
  3.3 44.3 %all_to_all.15 = bf16[64,2,8,1152]{3,2,1,0:T(8,128)(2,1)S(1)} all-to-all(bf16[64,2,8,1152]{3,2,1,0:T(8,128)(2,1)S(1)} %broadcast_in_dim.21), channel_id=1, replica_groups={{0,2,4,6,8,10,12,14,16,18,20,22,24,26,28,30,32,34,36,38,40,42,44,46,48,..., dimensions={0} | all-to-all | bytes 4718592 | tf_op jit(solution)/shard_map/all_to_all | solution.py:278
  47.7 1.6 copy.48
  52.9 4.6 %collective-permute-start.1 = (f32[3,32,4,128]{3,2,1,0:T(4,128)S(1)}, f32[3,32,4,128]{3,2,1,0:T(4,128)S(1)}, u32[]{:S(2)}, u32[]{:S(2)}) collective-permute-start(f32[3,32,4,128]{3,2,1,0:T(4,128)S(1)} %pad_maximum_fusion.4), channel_id=1, source_target_pairs={{0,8},{8,16},{16,24},{24,32},{32,40},{40,48},{48,56},{56,64},{64,7... | collective-permute-start | bytes 589832 | tf_op jit(solution)/shard_map/ppermute | solution.py:29
  57.5 13.3 %gather_fusion = bf16[1024,2048]{1,0:T(8,128)(2,1)} fusion(bf16[2048,2048]{1,0:T(8,128)(2,1)} %param.23, s32[1024]{0:T(1024)S(1)} %fusion.11), kind=kCustom, calls=%fused_computation | custom fusion | bytes 8392704 | tf_op jit(solution)/shard_map/gather | solution.py:394
  71.6 3.8 %pack_sides.1 = (f32[3,72,128]{2,1,0:T(8,128)}, f32[3,72,128]{2,1,0:T(8,128)}) custom-call(f32[32,64,128]{2,1,0:T(8,128)} %u_ref.3, f32[32,64,128]{2,1,0:T(8,128)} %k_ref.3, f32[32,64,128]{2,1,0:T(8,128)} %r_ref.3, f32[3,32,8,128]{3,2,1,0:T(8,128)} %pad_maximum_fusion.2.halo_ref), custom_call_target="tpu_custom_call" | custom-call | flops 16777216 | bytes 12582912 | tf_op jit(solution)/shard_map/pack_sides/pallas_call | solution.py:56
  76.7 3.2 %collective-permute-start.3 = (f32[3,72,128]{2,1,0:T(8,128)}, f32[3,72,128]{2,1,0:T(8,128)S(1)}, u32[]{:S(2)}, u32[]{:S(2)}) collective-permute-start(f32[3,72,128]{2,1,0:T(8,128)} %get-tuple-element.36), channel_id=1, source_target_pairs={{0,1},{1,2},{2,3},{3,4},{4,5},{5,6},{6,7},{8,9},{9,10},{10,11},{11... | collective-permute-start | bytes 331784 | tf_op jit(solution)/shard_map/ppermute | solution.py:29
  81.8 26.9 %solve.1 = (f32[32,64,128]{2,1,0:T(8,128)}, bf16[256,2048]{1,0:T(8,128)(2,1)}) custom-call(s32[4]{0:T(128)} %pad_add_fusion.pos_ref, f32[32,64,128]{2,1,0:T(8,128)} %u_ref.3, f32[32,64,128]{2,1,0:T(8,128)} %k_ref.3, f32[32,64,128]{2,1,0:T(8,128)} %r_ref.3, f32[3,32,8,128]{3,2,1,0:T(8,128)} %pad_maximum_fusion.2.halo_ref, f32[3,72,128]{2,1,0:T(8,128)} %copy-done.8, ...), custom_call_target="tpu_custom_call" | custom-call | flops 125829120 | bytes 67108864 | tf_op jit(solution)/shard_map/solve/pallas_call | solution.py:242
  108.7 1.7 convolution_convert_fusion
  110.4 2.1 select_bitcast_fusion.1
  113.0 2.2 copy-done.3
  115.7 7.4 %add_tanh_fusion = f32[1280,1024]{1,0:T(8,128)} fusion(f32[1024]{0:T(1024)S(1)} %add.146, bf16[2,1024,1152]{2,1,0:T(8,128)(2,1)} %bitcast.123, bf16[1024,2048]{1,0:T(8,128)(2,1)} %gather_fusion, bf16[256,2048]{1,0:T(8,128)(2,1)S(1)} %convolution_convert_fusion), kind=kOutput, calls=%fused_computation.5 | convolution fusion | flops 2690908160 | bytes 12587008 | tf_op jit(solution)/shard_map/dot_general | solution.py:399
  124.6 7.1 %fusion.21 = (f32[1024]{0:T(1024)S(1)}, bf16[1280,1024]{1,0:T(8,128)(2,1)S(1)}) fusion(f32[1280]{0:T(1024)S(1)} %pad_divide_fusion, bf16[256,2048]{1,0:T(8,128)(2,1)S(1)} %convolution_convert_fusion, bf16[1024,2048]{1,0:T(8,128)(2,1)} %gather_fusion, f32[1024]{0:T(1024)S(1)} %add.149, bf16[2,1024,1152]{2,1,0:T(8,128)(2,1)} %bitcast.124, ...), kind=kOutput, calls=%fused_computation.84 | convolution fusion | flops 2697460736 | bytes 15217664 | tf_op jit(solution)/shard_map/dot_general | solution.py:402
  131.8 4.9 %fusion.22 = (f32[1024]{0:T(1024)S(1)}, bf16[1280,1024]{1,0:T(8,128)(2,1)S(1)}) fusion(f32[1280,1024]{1,0:T(8,128)S(1)} %copy-done.18, bf16[2,1024,1152]{2,1,0:T(8,128)(2,1)} %bitcast.125, bf16[1280,1024]{1,0:T(8,128)(2,1)S(1)} %get-tuple-element.58), kind=kOutput, calls=%fused_computation.85 | convolution fusion | flops 2690907136 | bytes 12587008 | tf_op jit(solution)/shard_map/dot_general | solution.py:407
  136.6 4.5 %fusion.3 = f32[1024,1024]{1,0:T(8,128)} fusion(bf16[1280,1024]{1,0:T(8,128)(2,1)S(1)} %get-tuple-element.58, f32[1280,1024]{1,0:T(8,128)S(1)} %copy-done.18), kind=kOutput, calls=%fused_computation.24 | convolution fusion | flops 2685665280 | bytes 12058624 | tf_op jit(solution)/shard_map/dot_general | solution.py:405
  141.2 4.5 %fusion.1 = f32[1024,1024]{1,0:T(8,128)} fusion(bf16[1280,1024]{1,0:T(8,128)(2,1)S(1)} %get-tuple-element.60, bf16[1024,2048]{1,0:T(8,128)(2,1)S(1)} %copy-done.4, bf16[256,2048]{1,0:T(8,128)(2,1)S(1)} %convolution_convert_fusion), kind=kOutput, calls=%fused_computation.11 | convolution fusion | flops 2689597440 | bytes 12058624 | tf_op jit(solution)/shard_map/dot_general | solution.py:411
  146.2 3.3 %dynamic-slice_bitcast_fusion.1 = f32[64,64,128]{2,1,0:T(8,128)} fusion(f32[2,64,64,128]{3,2,0,1:T(8,128)} %bitcast.126, s32[]{:T(128)S(6)} %select_n.111), kind=kLoop, calls=%fused_computation.23 | loop fusion | bytes 4194308 | tf_op jit(solution)/shard_map/jit(dynamic_index_in_dim)/squeeze | solution.py:342
  149.6 1.8 collective-permute-start.8
  151.8 2.1 copy-done
  153.9 1.5 dynamic-slice_bitcast_fusion
  155.5 2.6 %bitcast_add_fusion.1 = f32[64,64,128]{2,1,0:T(8,128)S(1)} fusion(f32[64,64,128]{2,1,0:T(8,128)} %collective-permute-done.8, f32[2,64,64,128]{3,2,0,1:T(8,128)} %bitcast.127, s32[]{:T(128)S(6)} %select_n.110), kind=kLoop, calls=%fused_computation.21 | loop fusion | flops 524288 | bytes 6291460 | tf_op jit(solution)/shard_map/add | solution.py:345
  160.3 1.3 copy-done.1
  162.2 2.9 %collective-permute-start.6 = (f32[2,16,72,128]{3,2,0,1:T(8,128)S(1)}, f32[2,16,72,128]{3,2,0,1:T(8,128)}, u32[]{:S(2)}, u32[]{:S(2)}) collective-permute-start(f32[2,16,72,128]{3,2,0,1:T(8,128)S(1)} %dynamic-slice_bitcast_fusion.2), channel_id=1, source_target_pairs={{0,24},{1,7},{2,26},{3,5},{4,28},{5,3},{6,30},{7,1},{8,16},{9,15},... | collective-permute-start | bytes 3538952 | tf_op jit(solution)/shard_map/ppermute | solution.py:327
  165.1 10.8 %collective-permute-done.9 = f32[2,16,64,128]{3,2,1,0:T(8,128)} collective-permute-done((f32[2,16,64,128]{3,2,1,0:T(8,128)}, f32[2,16,64,128]{3,2,1,0:T(8,128)}, u32[]{:S(2)}, u32[]{:S(2)}) %collective-permute-start.9) | collective-permute-done | bytes 1048608 | tf_op jit(solution)/shard_map/ppermute | solution.py:327
  175.9 1.7 bitcast_add_fusion.3
  179.3 8.7 %collective-permute-done.6 = f32[2,16,72,128]{3,2,0,1:T(8,128)} collective-permute-done((f32[2,16,72,128]{3,2,0,1:T(8,128)S(1)}, f32[2,16,72,128]{3,2,0,1:T(8,128)}, u32[]{:S(2)}, u32[]{:S(2)}) %collective-permute-start.6) | collective-permute-done | bytes 1179680 | tf_op jit(solution)/shard_map/ppermute | solution.py:327
  188.0 1.4 bitcast_add_fusion.2
  189.6 2.1 bitcast_add_fusion.5
  191.7 8.1 %all-to-all-start.2 = ((f32[16,64,128]{2,1,0:T(8,128)}), f32[16,64,128]{2,1,0:T(8,128)S(1)}, u32[]{:S(2)}, u32[]{:S(2)}) async-start(f32[16,64,128]{2,1,0:T(8,128)} %bitcast_add_fusion.5), calls=%async_computation.2 | async-start | bytes 1048576 | tf_op jit(solution)/shard_map/all_to_all | solution.py:353
  199.8 2.1 collective-permute-done.7
  202.8 7.1 %all-to-all-done.2 = f32[16,64,128]{2,1,0:T(8,128)S(1)} async-done(((f32[16,64,128]{2,1,0:T(8,128)}), f32[16,64,128]{2,1,0:T(8,128)S(1)}, u32[]{:S(2)}, u32[]{:S(2)}) %all-to-all-start.2) | async-done | bytes 524320 | tf_op jit(solution)/shard_map/all_to_all | solution.py:353
  209.9 3.6 %all-to-all-start.1 = ((f32[16,72,128]{2,1,0:T(8,128)}), f32[16,72,128]{2,1,0:T(8,128)S(1)}, u32[]{:S(2)}, u32[]{:S(2)}) async-start(f32[16,72,128]{2,1,0:T(8,128)} %bitcast_add_fusion.4), calls=%async_computation.1 | async-start | bytes 1179648 | tf_op jit(solution)/shard_map/all_to_all | solution.py:353
  213.6 10.9 %all-to-all-done.1 = f32[16,72,128]{2,1,0:T(8,128)S(1)} async-done(((f32[16,72,128]{2,1,0:T(8,128)}), f32[16,72,128]{2,1,0:T(8,128)S(1)}, u32[]{:S(2)}, u32[]{:S(2)}) %all-to-all-start.1) | async-done | bytes 589856 | tf_op jit(solution)/shard_map/all_to_all | solution.py:353
  (97 shorter events, 20.6 us)
Async XLA Ops:
  47.7 9.8 %copy-start.12 = (s32[1024]{0:T(1024)S(1)}, s32[1024]{0:T(1024)}, u32[]{:S(2)}) copy-start(s32[1024]{0:T(1024)} %param.22) | copy-start | bytes 12292
  49.3 61.1 %collective-permute-start.4 = (bf16[64,2,8,1152]{3,2,0,1:T(8,128)(2,1)}, bf16[64,2,8,1152]{3,2,0,1:T(8,128)(2,1)}, u32[]{:S(2)}, u32[]{:S(2)}) collective-permute-start(bf16[64,2,8,1152]{3,2,0,1:T(8,128)(2,1)} %copy.48), channel_id=1, source_target_pairs={{0,1},{1,0},{2,3},{3,2},{4,5},{5,4},{6,7},{7,6},{8,9},{9,8},{10,11... | collective-permute-start | bytes 7077896 | tf_op jit(solution)/shard_map/ppermute | solution.py:274
  51.5 19.3 %collective-permute-start = (f32[3,32,4,128]{3,2,1,0:T(4,128)S(1)}, f32[3,32,4,128]{3,2,1,0:T(4,128)S(1)}, u32[]{:S(2)}, u32[]{:S(2)}) collective-permute-start(f32[3,32,4,128]{3,2,1,0:T(4,128)S(1)} %pad_maximum_fusion.3), channel_id=1, source_target_pairs={{8,0},{16,8},{24,16},{32,24},{40,32},{48,40},{56,48},{64,56},{72,6... | collective-permute-start | bytes 589832 | tf_op jit(solution)/shard_map/ppermute | solution.py:29
  52.9 17.9 %collective-permute-start.1 = (f32[3,32,4,128]{3,2,1,0:T(4,128)S(1)}, f32[3,32,4,128]{3,2,1,0:T(4,128)S(1)}, u32[]{:S(2)}, u32[]{:S(2)}) collective-permute-start(f32[3,32,4,128]{3,2,1,0:T(4,128)S(1)} %pad_maximum_fusion.4), channel_id=1, source_target_pairs={{0,8},{8,16},{16,24},{24,32},{32,40},{40,48},{48,56},{56,64},{64,7... | collective-permute-start | bytes 589832 | tf_op jit(solution)/shard_map/ppermute | solution.py:29
  57.5 13.3 %copy-start.16 = (s32[256]{0:T(256)S(1)}, s32[256]{0:T(256)}, u32[]{:S(2)}) copy-start(s32[256]{0:T(256)} %param.20) | copy-start | bytes 3076
  75.4 5.1 %collective-permute-start.2 = (f32[3,72,128]{2,1,0:T(8,128)}, f32[3,72,128]{2,1,0:T(8,128)S(1)}, u32[]{:S(2)}, u32[]{:S(2)}) collective-permute-start(f32[3,72,128]{2,1,0:T(8,128)} %get-tuple-element.35), channel_id=1, source_target_pairs={{1,0},{2,1},{3,2},{4,3},{5,4},{6,5},{7,6},{9,8},{10,9},{11,10},{12... | collective-permute-start | bytes 331784 | tf_op jit(solution)/shard_map/ppermute | solution.py:29
  76.7 4.2 %collective-permute-start.3 = (f32[3,72,128]{2,1,0:T(8,128)}, f32[3,72,128]{2,1,0:T(8,128)S(1)}, u32[]{:S(2)}, u32[]{:S(2)}) collective-permute-start(f32[3,72,128]{2,1,0:T(8,128)} %get-tuple-element.36), channel_id=1, source_target_pairs={{0,1},{1,2},{2,3},{3,4},{4,5},{5,6},{6,7},{8,9},{9,10},{10,11},{11... | collective-permute-start | bytes 331784 | tf_op jit(solution)/shard_map/ppermute | solution.py:29
  80.5 0.6 copy-start.8
  81.2 0.6 copy-start.9
  113.0 2.2 copy-start.3
  115.6 8.0 %copy-start.17 = (s32[256,1]{0,1:T(1,128)S(1)}, s32[256,1]{0,1:T(1,128)}, u32[]{:S(2)}) copy-start(s32[256,1]{0,1:T(1,128)} %param.21) | copy-start | bytes 3076
  124.6 7.1 %copy-start.18 = (f32[1280,1024]{1,0:T(8,128)S(1)}, f32[1280,1024]{1,0:T(8,128)}, u32[]{:S(2)}) copy-start(f32[1280,1024]{1,0:T(8,128)} %add_tanh_fusion) | copy-start | bytes 15728644
  136.6 4.5 %copy-start.4 = (bf16[1024,2048]{1,0:T(8,128)(2,1)S(1)}, bf16[1024,2048]{1,0:T(8,128)(2,1)}, u32[]{:S(2)}) copy-start(bf16[1024,2048]{1,0:T(8,128)(2,1)} %gather_fusion) | copy-start | bytes 12582916
  146.2 5.2 %copy-start.5 = (f32[1024,1024]{1,0:T(8,128)S(1)}, f32[1024,1024]{1,0:T(8,128)}, u32[]{:S(2)}) copy-start(f32[1024,1024]{1,0:T(8,128)} %fusion.1) | copy-start | bytes 12582916
  149.6 6.0 %collective-permute-start.8 = (f32[64,64,128]{2,1,0:T(8,128)}, f32[64,64,128]{2,1,0:T(8,128)}, u32[]{:S(2)}, u32[]{:S(2)}) collective-permute-start(f32[64,64,128]{2,1,0:T(8,128)} %dynamic-slice_bitcast_fusion.1), channel_id=1, source_target_pairs={{0,1},{1,0},{2,3},{3,2},{4,5},{5,4},{6,7},{7,6},{8,9},{9,8},{10,11... | collective-permute-start | bytes 6291464 | tf_op jit(solution)/shard_map/ppermute | solution.py:274
  151.8 2.1 copy-start
  155.5 4.8 %collective-permute-start.5 = (f32[64,72,128]{2,1,0:T(8,128)}, f32[64,72,128]{2,1,0:T(8,128)S(1)}, u32[]{:S(2)}, u32[]{:S(2)}) collective-permute-start(f32[64,72,128]{2,1,0:T(8,128)} %dynamic-slice_bitcast_fusion), channel_id=1, source_target_pairs={{0,1},{1,0},{2,3},{3,2},{4,5},{5,4},{6,7},{7,6},{8,9},{9,8},{10,11... | collective-permute-start | bytes 7077896 | tf_op jit(solution)/shard_map/ppermute | solution.py:274
  158.1 3.5 %copy-start.1 = (f32[2,64,72,128]{3,2,1,0:T(8,128)S(1)}, f32[2,64,72,128]{3,2,1,0:T(8,128)}, u32[]{:S(2)}) copy-start(f32[2,64,72,128]{3,2,1,0:T(8,128)} %copy-done) | copy-start | bytes 14155780
  158.4 1.9 copy-start.2
  159.5 16.3 %collective-permute-start.9 = (f32[2,16,64,128]{3,2,1,0:T(8,128)}, f32[2,16,64,128]{3,2,1,0:T(8,128)}, u32[]{:S(2)}, u32[]{:S(2)}) collective-permute-start(f32[2,16,64,128]{3,2,1,0:T(8,128)} %dynamic-slice_bitcast_fusion.3), channel_id=1, source_target_pairs={{0,96},{1,25},{2,98},{3,27},{4,100},{5,29},{6,102},{7,31},{8,104},... | collective-permute-start | bytes 3145736 | tf_op jit(solution)/shard_map/ppermute | solution.py:327
  162.2 25.8 %collective-permute-start.6 = (f32[2,16,72,128]{3,2,0,1:T(8,128)S(1)}, f32[2,16,72,128]{3,2,0,1:T(8,128)}, u32[]{:S(2)}, u32[]{:S(2)}) collective-permute-start(f32[2,16,72,128]{3,2,0,1:T(8,128)S(1)} %dynamic-slice_bitcast_fusion.2), channel_id=1, source_target_pairs={{0,24},{1,7},{2,26},{3,5},{4,28},{5,3},{6,30},{7,1},{8,16},{9,15},... | collective-permute-start | bytes 3538952 | tf_op jit(solution)/shard_map/ppermute | solution.py:327
  177.6 1.0 copy-start.6
  179.3 10.2 %collective-permute-start.10 = (f32[16,64,128]{2,1,0:T(8,128)}, f32[16,64,128]{2,1,0:T(8,128)}, u32[]{:S(2)}, u32[]{:S(2)}) collective-permute-start(f32[16,64,128]{2,1,0:T(8,128)} %dynamic-slice_bitcast_fusion.5), channel_id=1, source_target_pairs={{0,32},{1,9},{2,34},{3,11},{4,36},{5,13},{6,38},{7,15},{8,40},{9,1... | collective-permute-start | bytes 1572872 | tf_op jit(solution)/shard_map/ppermute | solution.py:327
  189.5 12.5 %collective-permute-start.7 = (f32[16,72,128]{2,1,0:T(8,128)S(1)}, f32[16,72,128]{2,1,0:T(8,128)S(1)}, u32[]{:S(2)}, u32[]{:S(2)}) collective-permute-start(f32[16,72,128]{2,1,0:T(8,128)S(1)} %dynamic-slice_bitcast_fusion.4), channel_id=1, source_target_pairs={{0,8},{1,3},{2,10},{3,1},{4,12},{5,7},{6,14},{7,5},{8,0},{9,11},{1... | collective-permute-start | bytes 1769480 | tf_op jit(solution)/shard_map/ppermute | solution.py:327
  191.7 32.8 %copy-start.13 = (f32[2,8]{1,0:T(2,128)S(1)}, f32[2,8]{1,0:T(2,128)}, u32[]{:S(2)}) copy-start(f32[2,8]{1,0:T(2,128)} %param.27) | copy-start | bytes 196
  191.7 32.8 %copy-start.14 = (f32[2,8]{1,0:T(2,128)S(1)}, f32[2,8]{1,0:T(2,128)}, u32[]{:S(2)}) copy-start(f32[2,8]{1,0:T(2,128)} %param.28) | copy-start | bytes 196
  191.7 32.8 %copy-start.15 = (f32[2,8]{1,0:T(2,128)S(1)}, f32[2,8]{1,0:T(2,128)}, u32[]{:S(2)}) copy-start(f32[2,8]{1,0:T(2,128)} %param.29) | copy-start | bytes 196
  191.7 33.4 %copy-start.7 = (f32[2,8,1024]{2,1,0:T(8,128)S(1)}, f32[2,8,1024]{2,1,0:T(8,128)}, u32[]{:S(2)}) copy-start(f32[2,8,1024]{2,1,0:T(8,128)} %param.24) | copy-start | bytes 196612
  191.7 33.4 %copy-start.10 = (f32[2,8,1024]{2,1,0:T(8,128)S(1)}, f32[2,8,1024]{2,1,0:T(8,128)}, u32[]{:S(2)}) copy-start(f32[2,8,1024]{2,1,0:T(8,128)} %param.25) | copy-start | bytes 196612
  191.7 33.4 %copy-start.11 = (f32[2,8,1024]{2,1,0:T(8,128)S(1)}, f32[2,8,1024]{2,1,0:T(8,128)}, u32[]{:S(2)}) copy-start(f32[2,8,1024]{2,1,0:T(8,128)} %param.26) | copy-start | bytes 196612
  191.7 18.2 %all-to-all-start.2 = ((f32[16,64,128]{2,1,0:T(8,128)}), f32[16,64,128]{2,1,0:T(8,128)S(1)}, u32[]{:S(2)}, u32[]{:S(2)}) async-start(f32[16,64,128]{2,1,0:T(8,128)} %bitcast_add_fusion.5), calls=%async_computation.2 | async-start | bytes 1048576 | tf_op jit(solution)/shard_map/all_to_all | solution.py:353
  209.9 14.5 %all-to-all-start.1 = ((f32[16,72,128]{2,1,0:T(8,128)}), f32[16,72,128]{2,1,0:T(8,128)S(1)}, u32[]{:S(2)}, u32[]{:S(2)}) async-start(f32[16,72,128]{2,1,0:T(8,128)} %bitcast_add_fusion.4), calls=%async_computation.1 | async-start | bytes 1179648 | tf_op jit(solution)/shard_map/all_to_all | solution.py:353

commit v2 on v1

--- a/solution.py
+++ b/solution.py
@@ -75,10 +75,11 @@
             table_ref[yb * cells_x : (yb + 1) * cells_x, pl.ds(at, 128)] = row.astype(jnp.bfloat16)
         return carry
 
-    lax.fori_loop(0, depth // per, body, 0)
+    lax.fori_loop(0, depth // per, body, 0, unroll=UNROLL)
 
 
 MARGIN = 8
+UNROLL = 4
 
 
 def solve_kernel(
@@ -97,6 +98,7 @@
     rr,
     cx,
     cy,
+    cl,
     cz,
     dt_ref,
 ):
@@ -152,28 +154,27 @@
         for t in range(tiles):
             k = [kk[w, z + 1, rows(t), :] for w in range(2)]
             after = turned(k, False)
+            before = turned(k, True)
             for w in range(2):
-                cz[w, z, rows(t), :] = half * (kk[w, z, rows(t), :] + k[w])
-                cx[w, z, rows(t), :] = half * (k[w] + kk[w, z + 1, rows(t, 1), :])
-                cy[w, z, rows(t), :] = half * (k[w] + after[w])
+                ahead = half * (k[w] + kk[w, z + 1, rows(t, 1), :])
+                cx[w, z, rows(t), :] = ahead
+                if t == 0:
+                    continue
+                low = half * (kk[w, z, rows(t), :] + k[w])
+                cz[w, z, rows(t), :] = low
+                right = half * (k[w] + after[w])
+                left = half * (k[w] + before[w])
+                cy[w, z, rows(t), :] = right
+                cl[w, z, rows(t), :] = left
+                loss = low + half * (k[w] + kk[w, z + 2, rows(t), :])
+                loss = loss + (ahead + half * (k[w] + kk[w, z + 1, rows(t, -1), :]))
+                loss = loss + (right + left)
+                rr[w, z, rows(t), :] = (1.0 - time_step * rr[w, z, rows(t), :]) - loss
         return carry
 
-    lax.fori_loop(0, depth, faces, 0)
+    lax.fori_loop(0, depth, faces, 0, unroll=UNROLL)
     for w in range(2):
         cz[w, depth] = half * kk[w, depth]
-
-    def keeps(z, carry):
-        for t in range(halo_top // 8, tiles):
-            ys = [cy[w, z, rows(t), :] for w in range(2)]
-            back = turned(ys, True)
-            for w in range(2):
-                loss = cz[w, z + 1, rows(t), :] + cz[w, z, rows(t), :]
-                loss = loss + (cx[w, z, rows(t), :] + cx[w, z, rows(t, -1), :])
-                loss = loss + (ys[w] + back[w])
-                rr[w, z, rows(t), :] = (1.0 - time_step * rr[w, z, rows(t), :]) - loss
-        return carry
-
-    lax.fori_loop(0, depth, keeps, 0)
 
     gx, gy = pos_ref[0], pos_ref[1]
     below = jnp.where(gx < pos_ref[2] - 1, 1, 0)
@@ -197,14 +198,14 @@
             for t in range(first_tile, end_tile):
                 u = [src[w, z + 1, rows(t), :] for w in range(2)]
                 after = turned(u, False)
-                ys = [cy[w, z, rows(t), :] for w in range(2)]
-                back = turned([ys[w] * u[w] for w in range(2)], True)
+                before = turned(u, True)
                 for w in picks:
                     total = cz[w, z + 1, rows(t), :] * src[w, z + 2, rows(t), :]
                     total = total + cz[w, z, rows(t), :] * src[w, z, rows(t), :]
                     total = total + cx[w, z, rows(t), :] * src[w, z + 1, rows(t, 1), :]
                     total = total + cx[w, z, rows(t, -1), :] * src[w, z + 1, rows(t, -1), :]
-                    total = total + (ys[w] * after[w] + back[w])
+                    total = total + cy[w, z, rows(t), :] * after[w]
+                    total = total + cl[w, z, rows(t), :] * before[w]
                     total = total + rr[w, z, rows(t), :] * u[w]
                     if last:
                         out_ref[z, rows(t - main // 8), :] = total
@@ -214,7 +215,7 @@
                         dst[w, z + 1, rows(t), :] = dt_ref[w, rows(t), :] * total
             return carry
 
-        lax.fori_loop(0, depth, body, 0)
+        lax.fori_loop(0, depth, body, 0, unroll=UNROLL)
 
     src, dst = ua, ub
     for step in range(STEPS):
@@ -248,7 +249,7 @@
         in_specs=[pl.BlockSpec(memory_space=pltpu.SMEM)]
         + [pl.BlockSpec(memory_space=pltpu.VMEM)] * 6,
         out_specs=(pl.BlockSpec(memory_space=pltpu.VMEM),) * 2,
-        scratch_shapes=[padded, padded, padded, whole, whole, whole,
+        scratch_shapes=[padded, padded, padded, whole, whole, whole, whole,
             pltpu.VMEM((2, depth + 1, rows, lanes), jnp.float32),
             pltpu.VMEM((2, rows, lanes), jnp.float32)],
         cost_estimate=pl.CostEstimate(

time: 230 us -> 220 us (0.957)
  Pallas kernels: 30.7 us -> 19.8 us
    pallas_call x1, Pallas kernels: 26.9 us -> 16.1 us  [solve(): pl.pallas_call(solve_kernel, out_shape=(jax.ShapeDtypeStruct(field.shape,...]
  transfers between devices with their start and end apart: 13 -> 13, of which waited for: 6 -> 6; matrix products, arithmetic and copies ran while one was open for 14% -> 15% of each run, Pallas kernels for 14% -> 9%
where the time goes in v2:
time: 220 us; the launch traced here: 215 us
  blocking collectives  44.3 us (20%)
  waiting for transfers between devices  39.9 us (18%)
  local copies, waits for them, and re-layouts  32.8 us (15%)
  matrix products  30.3 us (14%)
  starting transfers between devices  27.6 us (13%)
  Pallas kernels  19.8 us (9%)
  other arithmetic  19.2 us (9%)
    all_to_all x1, blocking collectives, chips_all_to_all(): lax.all_to_all(x, AXES, 0, 0, tiled=True, axis_index_groups=chip_groups(d...  44.3 us
    ppermute x4, waiting for transfers between devices, halve(): return keep + lax.ppermute(send, AXES, pairs)  21.6 us
    all_to_all x2, waiting for transfers between devices, reduce_parts(): got = lax.all_to_all(mine, AXES, 0, 0, tiled=True, axis_index_groups=groups)  18 us
    pallas_call x1, Pallas kernels, solve(): pl.pallas_call(solve_kernel, out_shape=(jax.ShapeDtypeStruct(field.shape,...  16.1 us
    gather x1, local copies, waits for them, and re-layouts, step_all(): stored = reservoir[res_slot]  13.3 us
    all_to_all x2, starting transfers between devices, reduce_parts(): got = lax.all_to_all(mine, AXES, 0, 0, tiled=True, axis_index_groups=groups)  11.7 us
    ppermute x4, starting transfers between devices, exchange(): return (lax.ppermute(first, axis, down), lax.ppermute(last, axis, up))  10.3 us
    unnamed x39, local copies, waits for them, and re-layouts  7.64 us
  transfers between devices with their start and end apart: 13, of which 6 were waited for; matrix products, arithmetic and copies ran while one was open for 15% of the time, Pallas kernels for 9%

profile of v2, /device:TPU:0, one launch (start us, length us, event | category | flops | bytes accessed | tf_op | source)
XLA Modules:
  0.0 215.2 jit_solution(6887731801027545274)
XLA Ops:
  3.3 44.3 %all_to_all.15 = bf16[64,2,8,1152]{3,2,1,0:T(8,128)(2,1)S(1)} all-to-all(bf16[64,2,8,1152]{3,2,1,0:T(8,128)(2,1)S(1)} %broadcast_in_dim.21), channel_id=1, replica_groups={{0,2,4,6,8,10,12,14,16,18,20,22,24,26,28,30,32,34,36,38,40,42,44,46,48,..., dimensions={0} | all-to-all | bytes 4718592 | tf_op jit(solution)/shard_map/all_to_all | solution.py:279
  47.7 1.6 copy.48
  52.9 4.6 %collective-permute-start.1 = (f32[3,32,4,128]{3,2,1,0:T(4,128)S(1)}, f32[3,32,4,128]{3,2,1,0:T(4,128)S(1)}, u32[]{:S(2)}, u32[]{:S(2)}) collective-permute-start(f32[3,32,4,128]{3,2,1,0:T(4,128)S(1)} %pad_maximum_fusion.4), channel_id=1, source_target_pairs={{0,8},{8,16},{16,24},{24,32},{32,40},{40,48},{48,56},{56,64},{64,7... | collective-permute-start | bytes 589832 | tf_op jit(solution)/shard_map/ppermute | solution.py:29
  57.5 13.3 %gather_fusion = bf16[1024,2048]{1,0:T(8,128)(2,1)} fusion(bf16[2048,2048]{1,0:T(8,128)(2,1)} %param.23, s32[1024]{0:T(1024)S(1)} %fusion.11), kind=kCustom, calls=%fused_computation | custom fusion | bytes 8392704 | tf_op jit(solution)/shard_map/gather | solution.py:395
  71.6 3.8 %pack_sides.1 = (f32[3,72,128]{2,1,0:T(8,128)}, f32[3,72,128]{2,1,0:T(8,128)}) custom-call(f32[32,64,128]{2,1,0:T(8,128)} %u_ref.3, f32[32,64,128]{2,1,0:T(8,128)} %k_ref.3, f32[32,64,128]{2,1,0:T(8,128)} %r_ref.3, f32[3,32,8,128]{3,2,1,0:T(8,128)} %pad_maximum_fusion.2.halo_ref), custom_call_target="tpu_custom_call" | custom-call | flops 16777216 | bytes 12582912 | tf_op jit(solution)/shard_map/pack_sides/pallas_call | solution.py:56
  76.7 3.2 %collective-permute-start.3 = (f32[3,72,128]{2,1,0:T(8,128)}, f32[3,72,128]{2,1,0:T(8,128)S(1)}, u32[]{:S(2)}, u32[]{:S(2)}) collective-permute-start(f32[3,72,128]{2,1,0:T(8,128)} %get-tuple-element.36), channel_id=1, source_target_pairs={{0,1},{1,2},{2,3},{3,4},{4,5},{5,6},{6,7},{8,9},{9,10},{10,11},{11... | collective-permute-start | bytes 331784 | tf_op jit(solution)/shard_map/ppermute | solution.py:29
  81.8 16.1 %solve.1 = (f32[32,64,128]{2,1,0:T(8,128)}, bf16[256,2048]{1,0:T(8,128)(2,1)}) custom-call(s32[4]{0:T(128)} %pad_add_fusion.pos_ref, f32[32,64,128]{2,1,0:T(8,128)} %u_ref.3, f32[32,64,128]{2,1,0:T(8,128)} %k_ref.3, f32[32,64,128]{2,1,0:T(8,128)} %r_ref.3, f32[3,32,8,128]{3,2,1,0:T(8,128)} %pad_maximum_fusion.2.halo_ref, f32[3,72,128]{2,1,0:T(8,128)} %copy-done.8, ...), custom_call_target="tpu_custom_call" | custom-call | flops 125829120 | bytes 67108864 | tf_op jit(solution)/shard_map/solve/pallas_call | solution.py:243
  97.8 1.7 convolution_convert_fusion
  99.6 2.1 select_bitcast_fusion.1
  102.2 2.2 %copy-done.3 = bf16[64,2,2,8,1152]{4,3,1,0,2:T(8,128)(2,1)} copy-done((bf16[64,2,2,8,1152]{4,3,1,0,2:T(8,128)(2,1)}, bf16[64,2,2,8,1152]{4,3,1,0,2:T(8,128)(2,1)S(1)}, u32[]{:S(2)}) %copy-start.3) | copy-done | bytes 4718616
  104.8 7.4 %add_tanh_fusion = f32[1280,1024]{1,0:T(8,128)} fusion(f32[1024]{0:T(1024)S(1)} %add.146, bf16[2,1024,1152]{2,1,0:T(8,128)(2,1)} %bitcast.123, bf16[1024,2048]{1,0:T(8,128)(2,1)} %gather_fusion, bf16[256,2048]{1,0:T(8,128)(2,1)S(1)} %convolution_convert_fusion), kind=kOutput, calls=%fused_computation.5 | convolution fusion | flops 2690908160 | bytes 12587008 | tf_op jit(solution)/shard_map/dot_general | solution.py:400
  113.8 7.1 %fusion.21 = (f32[1024]{0:T(1024)S(1)}, bf16[1280,1024]{1,0:T(8,128)(2,1)S(1)}) fusion(f32[1280]{0:T(1024)S(1)} %pad_divide_fusion, bf16[256,2048]{1,0:T(8,128)(2,1)S(1)} %convolution_convert_fusion, bf16[1024,2048]{1,0:T(8,128)(2,1)} %gather_fusion, f32[1024]{0:T(1024)S(1)} %add.149, bf16[2,1024,1152]{2,1,0:T(8,128)(2,1)} %bitcast.124, ...), kind=kOutput, calls=%fused_computation.84 | convolution fusion | flops 2697460736 | bytes 15217664 | tf_op jit(solution)/shard_map/dot_general | solution.py:403
  120.9 4.9 %fusion.22 = (f32[1024]{0:T(1024)S(1)}, bf16[1280,1024]{1,0:T(8,128)(2,1)S(1)}) fusion(f32[1280,1024]{1,0:T(8,128)S(1)} %copy-done.18, bf16[2,1024,1152]{2,1,0:T(8,128)(2,1)} %bitcast.125, bf16[1280,1024]{1,0:T(8,128)(2,1)S(1)} %get-tuple-element.58), kind=kOutput, calls=%fused_computation.85 | convolution fusion | flops 2690907136 | bytes 12587008 | tf_op jit(solution)/shard_map/dot_general | solution.py:408
  125.8 4.7 %fusion.3 = f32[1024,1024]{1,0:T(8,128)} fusion(bf16[1280,1024]{1,0:T(8,128)(2,1)S(1)} %get-tuple-element.58, f32[1280,1024]{1,0:T(8,128)S(1)} %copy-done.18), kind=kOutput, calls=%fused_computation.24 | convolution fusion | flops 2685665280 | bytes 12058624 | tf_op jit(solution)/shard_map/dot_general | solution.py:406
  130.5 4.5 %fusion.1 = f32[1024,1024]{1,0:T(8,128)} fusion(bf16[1280,1024]{1,0:T(8,128)(2,1)S(1)} %get-tuple-element.60, bf16[1024,2048]{1,0:T(8,128)(2,1)S(1)} %copy-done.4, bf16[256,2048]{1,0:T(8,128)(2,1)S(1)} %convolution_convert_fusion), kind=kOutput, calls=%fused_computation.11 | convolution fusion | flops 2689597440 | bytes 12058624 | tf_op jit(solution)/shard_map/dot_general | solution.py:412
  135.6 3.3 %dynamic-slice_bitcast_fusion.1 = f32[64,64,128]{2,1,0:T(8,128)} fusion(f32[2,64,64,128]{3,2,0,1:T(8,128)} %bitcast.126, s32[]{:T(128)S(6)} %select_n.111), kind=kLoop, calls=%fused_computation.23 | loop fusion | bytes 4194308 | tf_op jit(solution)/shard_map/jit(dynamic_index_in_dim)/squeeze | solution.py:343
  138.9 1.8 collective-permute-start.8
  141.2 2.1 copy-done
  143.3 1.5 dynamic-slice_bitcast_fusion
  144.9 2.6 %bitcast_add_fusion.1 = f32[64,64,128]{2,1,0:T(8,128)S(1)} fusion(f32[64,64,128]{2,1,0:T(8,128)} %collective-permute-done.8, f32[2,64,64,128]{3,2,0,1:T(8,128)} %bitcast.127, s32[]{:T(128)S(6)} %select_n.110), kind=kLoop, calls=%fused_computation.21 | loop fusion | flops 524288 | bytes 6291460 | tf_op jit(solution)/shard_map/add | solution.py:346
  149.7 1.3 copy-done.1
  151.6 2.9 %collective-permute-start.6 = (f32[2,16,72,128]{3,2,0,1:T(8,128)S(1)}, f32[2,16,72,128]{3,2,0,1:T(8,128)}, u32[]{:S(2)}, u32[]{:S(2)}) collective-permute-start(f32[2,16,72,128]{3,2,0,1:T(8,128)S(1)} %dynamic-slice_bitcast_fusion.2), channel_id=1, source_target_pairs={{0,24},{1,7},{2,26},{3,5},{4,28},{5,3},{6,30},{7,1},{8,16},{9,15},... | collective-permute-start | bytes 3538952 | tf_op jit(solution)/shard_map/ppermute | solution.py:328
  154.5 10.7 %collective-permute-done.9 = f32[2,16,64,128]{3,2,1,0:T(8,128)} collective-permute-done((f32[2,16,64,128]{3,2,1,0:T(8,128)}, f32[2,16,64,128]{3,2,1,0:T(8,128)}, u32[]{:S(2)}, u32[]{:S(2)}) %collective-permute-start.9) | collective-permute-done | bytes 1048608 | tf_op jit(solution)/shard_map/ppermute | solution.py:328
  165.2 1.7 bitcast_add_fusion.3
  168.7 8.7 %collective-permute-done.6 = f32[2,16,72,128]{3,2,0,1:T(8,128)} collective-permute-done((f32[2,16,72,128]{3,2,0,1:T(8,128)S(1)}, f32[2,16,72,128]{3,2,0,1:T(8,128)}, u32[]{:S(2)}, u32[]{:S(2)}) %collective-permute-start.6) | collective-permute-done | bytes 1179680 | tf_op jit(solution)/shard_map/ppermute | solution.py:328
  177.4 1.4 bitcast_add_fusion.2
  178.9 2.1 bitcast_add_fusion.5
  181.1 8.1 %all-to-all-start.2 = ((f32[16,64,128]{2,1,0:T(8,128)}), f32[16,64,128]{2,1,0:T(8,128)S(1)}, u32[]{:S(2)}, u32[]{:S(2)}) async-start(f32[16,64,128]{2,1,0:T(8,128)} %bitcast_add_fusion.5), calls=%async_computation.2 | async-start | bytes 1048576 | tf_op jit(solution)/shard_map/all_to_all | solution.py:354
  189.2 2.1 collective-permute-done.7
  192.2 7.1 %all-to-all-done.2 = f32[16,64,128]{2,1,0:T(8,128)S(1)} async-done(((f32[16,64,128]{2,1,0:T(8,128)}), f32[16,64,128]{2,1,0:T(8,128)S(1)}, u32[]{:S(2)}, u32[]{:S(2)}) %all-to-all-start.2) | async-done | bytes 524320 | tf_op jit(solution)/shard_map/all_to_all | solution.py:354
  199.3 3.6 %all-to-all-start.1 = ((f32[16,72,128]{2,1,0:T(8,128)}), f32[16,72,128]{2,1,0:T(8,128)S(1)}, u32[]{:S(2)}, u32[]{:S(2)}) async-start(f32[16,72,128]{2,1,0:T(8,128)} %bitcast_add_fusion.4), calls=%async_computation.1 | async-start | bytes 1179648 | tf_op jit(solution)/shard_map/all_to_all | solution.py:354
  202.9 10.9 %all-to-all-done.1 = f32[16,72,128]{2,1,0:T(8,128)S(1)} async-done(((f32[16,72,128]{2,1,0:T(8,128)}), f32[16,72,128]{2,1,0:T(8,128)S(1)}, u32[]{:S(2)}, u32[]{:S(2)}) %all-to-all-start.1) | async-done | bytes 589856 | tf_op jit(solution)/shard_map/all_to_all | solution.py:354
  (97 shorter events, 20.6 us)
Async XLA Ops:
  47.7 9.8 %copy-start.12 = (s32[1024]{0:T(1024)S(1)}, s32[1024]{0:T(1024)}, u32[]{:S(2)}) copy-start(s32[1024]{0:T(1024)} %param.22) | copy-start | bytes 12292
  49.3 50.3 %collective-permute-start.4 = (bf16[64,2,8,1152]{3,2,0,1:T(8,128)(2,1)}, bf16[64,2,8,1152]{3,2,0,1:T(8,128)(2,1)}, u32[]{:S(2)}, u32[]{:S(2)}) collective-permute-start(bf16[64,2,8,1152]{3,2,0,1:T(8,128)(2,1)} %copy.48), channel_id=1, source_target_pairs={{0,1},{1,0},{2,3},{3,2},{4,5},{5,4},{6,7},{7,6},{8,9},{9,8},{10,11... | collective-permute-start | bytes 7077896 | tf_op jit(solution)/shard_map/ppermute | solution.py:275
  51.5 19.3 %collective-permute-start = (f32[3,32,4,128]{3,2,1,0:T(4,128)S(1)}, f32[3,32,4,128]{3,2,1,0:T(4,128)S(1)}, u32[]{:S(2)}, u32[]{:S(2)}) collective-permute-start(f32[3,32,4,128]{3,2,1,0:T(4,128)S(1)} %pad_maximum_fusion.3), channel_id=1, source_target_pairs={{8,0},{16,8},{24,16},{32,24},{40,32},{48,40},{56,48},{64,56},{72,6... | collective-permute-start | bytes 589832 | tf_op jit(solution)/shard_map/ppermute | solution.py:29
  52.9 17.9 %collective-permute-start.1 = (f32[3,32,4,128]{3,2,1,0:T(4,128)S(1)}, f32[3,32,4,128]{3,2,1,0:T(4,128)S(1)}, u32[]{:S(2)}, u32[]{:S(2)}) collective-permute-start(f32[3,32,4,128]{3,2,1,0:T(4,128)S(1)} %pad_maximum_fusion.4), channel_id=1, source_target_pairs={{0,8},{8,16},{16,24},{24,32},{32,40},{40,48},{48,56},{56,64},{64,7... | collective-permute-start | bytes 589832 | tf_op jit(solution)/shard_map/ppermute | solution.py:29
  57.5 13.3 %copy-start.16 = (s32[256]{0:T(256)S(1)}, s32[256]{0:T(256)}, u32[]{:S(2)}) copy-start(s32[256]{0:T(256)} %param.20) | copy-start | bytes 3076
  75.4 5.1 %collective-permute-start.2 = (f32[3,72,128]{2,1,0:T(8,128)}, f32[3,72,128]{2,1,0:T(8,128)S(1)}, u32[]{:S(2)}, u32[]{:S(2)}) collective-permute-start(f32[3,72,128]{2,1,0:T(8,128)} %get-tuple-element.35), channel_id=1, source_target_pairs={{1,0},{2,1},{3,2},{4,3},{5,4},{6,5},{7,6},{9,8},{10,9},{11,10},{12... | collective-permute-start | bytes 331784 | tf_op jit(solution)/shard_map/ppermute | solution.py:29
  76.7 4.2 %collective-permute-start.3 = (f32[3,72,128]{2,1,0:T(8,128)}, f32[3,72,128]{2,1,0:T(8,128)S(1)}, u32[]{:S(2)}, u32[]{:S(2)}) collective-permute-start(f32[3,72,128]{2,1,0:T(8,128)} %get-tuple-element.36), channel_id=1, source_target_pairs={{0,1},{1,2},{2,3},{3,4},{4,5},{5,6},{6,7},{8,9},{9,10},{10,11},{11... | collective-permute-start | bytes 331784 | tf_op jit(solution)/shard_map/ppermute | solution.py:29
  80.5 0.6 copy-start.8
  81.2 0.6 copy-start.9
  102.1 2.2 %copy-start.3 = (bf16[64,2,2,8,1152]{4,3,1,0,2:T(8,128)(2,1)}, bf16[64,2,2,8,1152]{4,3,1,0,2:T(8,128)(2,1)S(1)}, u32[]{:S(2)}) copy-start(bf16[64,2,2,8,1152]{4,3,1,0,2:T(8,128)(2,1)S(1)} %pad_maximum_fusion) | copy-start | bytes 14155780
  104.8 8.0 %copy-start.17 = (s32[256,1]{0,1:T(1,128)S(1)}, s32[256,1]{0,1:T(1,128)}, u32[]{:S(2)}) copy-start(s32[256,1]{0,1:T(1,128)} %param.21) | copy-start | bytes 3076
  113.8 7.1 %copy-start.18 = (f32[1280,1024]{1,0:T(8,128)S(1)}, f32[1280,1024]{1,0:T(8,128)}, u32[]{:S(2)}) copy-start(f32[1280,1024]{1,0:T(8,128)} %add_tanh_fusion) | copy-start | bytes 15728644
  125.8 4.8 %copy-start.4 = (bf16[1024,2048]{1,0:T(8,128)(2,1)S(1)}, bf16[1024,2048]{1,0:T(8,128)(2,1)}, u32[]{:S(2)}) copy-start(bf16[1024,2048]{1,0:T(8,128)(2,1)} %gather_fusion) | copy-start | bytes 12582916
  135.6 5.2 %copy-start.5 = (f32[1024,1024]{1,0:T(8,128)S(1)}, f32[1024,1024]{1,0:T(8,128)}, u32[]{:S(2)}) copy-start(f32[1024,1024]{1,0:T(8,128)} %fusion.1) | copy-start | bytes 12582916
  138.9 6.0 %collective-permute-start.8 = (f32[64,64,128]{2,1,0:T(8,128)}, f32[64,64,128]{2,1,0:T(8,128)}, u32[]{:S(2)}, u32[]{:S(2)}) collective-permute-start(f32[64,64,128]{2,1,0:T(8,128)} %dynamic-slice_bitcast_fusion.1), channel_id=1, source_target_pairs={{0,1},{1,0},{2,3},{3,2},{4,5},{5,4},{6,7},{7,6},{8,9},{9,8},{10,11... | collective-permute-start | bytes 6291464 | tf_op jit(solution)/shard_map/ppermute | solution.py:275
  141.2 2.1 copy-start
  144.8 4.8 %collective-permute-start.5 = (f32[64,72,128]{2,1,0:T(8,128)}, f32[64,72,128]{2,1,0:T(8,128)S(1)}, u32[]{:S(2)}, u32[]{:S(2)}) collective-permute-start(f32[64,72,128]{2,1,0:T(8,128)} %dynamic-slice_bitcast_fusion), channel_id=1, source_target_pairs={{0,1},{1,0},{2,3},{3,2},{4,5},{5,4},{6,7},{7,6},{8,9},{9,8},{10,11... | collective-permute-start | bytes 7077896 | tf_op jit(solution)/shard_map/ppermute | solution.py:275
  147.5 3.5 %copy-start.1 = (f32[2,64,72,128]{3,2,1,0:T(8,128)S(1)}, f32[2,64,72,128]{3,2,1,0:T(8,128)}, u32[]{:S(2)}) copy-start(f32[2,64,72,128]{3,2,1,0:T(8,128)} %copy-done) | copy-start | bytes 14155780
  147.8 1.9 copy-start.2
  148.9 16.3 %collective-permute-start.9 = (f32[2,16,64,128]{3,2,1,0:T(8,128)}, f32[2,16,64,128]{3,2,1,0:T(8,128)}, u32[]{:S(2)}, u32[]{:S(2)}) collective-permute-start(f32[2,16,64,128]{3,2,1,0:T(8,128)} %dynamic-slice_bitcast_fusion.3), channel_id=1, source_target_pairs={{0,96},{1,25},{2,98},{3,27},{4,100},{5,29},{6,102},{7,31},{8,104},... | collective-permute-start | bytes 3145736 | tf_op jit(solution)/shard_map/ppermute | solution.py:328
  151.6 25.8 %collective-permute-start.6 = (f32[2,16,72,128]{3,2,0,1:T(8,128)S(1)}, f32[2,16,72,128]{3,2,0,1:T(8,128)}, u32[]{:S(2)}, u32[]{:S(2)}) collective-permute-start(f32[2,16,72,128]{3,2,0,1:T(8,128)S(1)} %dynamic-slice_bitcast_fusion.2), channel_id=1, source_target_pairs={{0,24},{1,7},{2,26},{3,5},{4,28},{5,3},{6,30},{7,1},{8,16},{9,15},... | collective-permute-start | bytes 3538952 | tf_op jit(solution)/shard_map/ppermute | solution.py:328
  166.9 1.0 copy-start.6
  168.7 10.2 %collective-permute-start.10 = (f32[16,64,128]{2,1,0:T(8,128)}, f32[16,64,128]{2,1,0:T(8,128)}, u32[]{:S(2)}, u32[]{:S(2)}) collective-permute-start(f32[16,64,128]{2,1,0:T(8,128)} %dynamic-slice_bitcast_fusion.5), channel_id=1, source_target_pairs={{0,32},{1,9},{2,34},{3,11},{4,36},{5,13},{6,38},{7,15},{8,40},{9,1... | collective-permute-start | bytes 1572872 | tf_op jit(solution)/shard_map/ppermute | solution.py:328
  178.8 12.5 %collective-permute-start.7 = (f32[16,72,128]{2,1,0:T(8,128)S(1)}, f32[16,72,128]{2,1,0:T(8,128)S(1)}, u32[]{:S(2)}, u32[]{:S(2)}) collective-permute-start(f32[16,72,128]{2,1,0:T(8,128)S(1)} %dynamic-slice_bitcast_fusion.4), channel_id=1, source_target_pairs={{0,8},{1,3},{2,10},{3,1},{4,12},{5,7},{6,14},{7,5},{8,0},{9,11},{1... | collective-permute-start | bytes 1769480 | tf_op jit(solution)/shard_map/ppermute | solution.py:328
  181.0 32.8 %copy-start.13 = (f32[2,8]{1,0:T(2,128)S(1)}, f32[2,8]{1,0:T(2,128)}, u32[]{:S(2)}) copy-start(f32[2,8]{1,0:T(2,128)} %param.27) | copy-start | bytes 196
  181.0 32.8 %copy-start.14 = (f32[2,8]{1,0:T(2,128)S(1)}, f32[2,8]{1,0:T(2,128)}, u32[]{:S(2)}) copy-start(f32[2,8]{1,0:T(2,128)} %param.28) | copy-start | bytes 196
  181.0 32.8 %copy-start.15 = (f32[2,8]{1,0:T(2,128)S(1)}, f32[2,8]{1,0:T(2,128)}, u32[]{:S(2)}) copy-start(f32[2,8]{1,0:T(2,128)} %param.29) | copy-start | bytes 196
  181.0 33.4 %copy-start.7 = (f32[2,8,1024]{2,1,0:T(8,128)S(1)}, f32[2,8,1024]{2,1,0:T(8,128)}, u32[]{:S(2)}) copy-start(f32[2,8,1024]{2,1,0:T(8,128)} %param.24) | copy-start | bytes 196612
  181.0 33.4 %copy-start.10 = (f32[2,8,1024]{2,1,0:T(8,128)S(1)}, f32[2,8,1024]{2,1,0:T(8,128)}, u32[]{:S(2)}) copy-start(f32[2,8,1024]{2,1,0:T(8,128)} %param.25) | copy-start | bytes 196612
  181.0 33.4 %copy-start.11 = (f32[2,8,1024]{2,1,0:T(8,128)S(1)}, f32[2,8,1024]{2,1,0:T(8,128)}, u32[]{:S(2)}) copy-start(f32[2,8,1024]{2,1,0:T(8,128)} %param.26) | copy-start | bytes 196612
  181.1 18.2 %all-to-all-start.2 = ((f32[16,64,128]{2,1,0:T(8,128)}), f32[16,64,128]{2,1,0:T(8,128)S(1)}, u32[]{:S(2)}, u32[]{:S(2)}) async-start(f32[16,64,128]{2,1,0:T(8,128)} %bitcast_add_fusion.5), calls=%async_computation.2 | async-start | bytes 1048576 | tf_op jit(solution)/shard_map/all_to_all | solution.py:354
  199.3 14.5 %all-to-all-start.1 = ((f32[16,72,128]{2,1,0:T(8,128)}), f32[16,72,128]{2,1,0:T(8,128)S(1)}, u32[]{:S(2)}, u32[]{:S(2)}) async-start(f32[16,72,128]{2,1,0:T(8,128)} %bitcast_add_fusion.4), calls=%async_computation.1 | async-start | bytes 1179648 | tf_op jit(solution)/shard_map/all_to_all | solution.py:354

commit v3 on v2

--- a/solution.py
+++ b/solution.py
@@ -318,6 +318,7 @@
 
 
 FAR_BIT = (6, 4, 2)
+TURNS = (0, 1)
 
 
 def halve(x, me, core, shifts, mask):
@@ -350,6 +351,10 @@
     near = [bit - 1 for bit in far]
     mine = halve(mine, me, core, far, [3 << bit for bit in near])
     mine = halve(mine, me, core, near, [1 << bit for bit in near])
+    return mine
+
+
+def spread(mine, axes):
     groups = axis_groups(axes[0], 0) + axis_groups(axes[1], 1)
     got = lax.all_to_all(mine, AXES, 0, 0, tiled=True, axis_index_groups=groups)
     return jnp.sum(got, 0)
@@ -404,7 +409,7 @@
     grad_pred = (pred - target) * scale
     grad_pred_b = grad_pred.astype(jnp.bfloat16)
     grad_w2 = jnp.dot(hidden_b.T, grad_pred_b, preferred_element_type=jnp.float32)
-    share_w2 = reduce_parts(chunks(grad_w2, devices), me, core, devices, (0, 1))
+    share_w2 = reduce_parts(chunks(grad_w2, devices), me, core, devices, TURNS)
     grad_hid = jnp.dot(grad_pred_b, wfull[1].T, preferred_element_type=jnp.float32)
     grad_pre = grad_hid * (1.0 - hidden * hidden)
     grad_pre_b = grad_pre.astype(jnp.bfloat16)
@@ -414,7 +419,9 @@
     tile_b = grad_b.reshape(2, devices // 2, 2, own).transpose(2, 1, 0, 3)
     tile_b = jnp.pad(tile_b, ((0, 0), (0, 0), (0, 8 - 2), (0, 128 - own)))
     parts = jnp.concatenate([chunks(grad_w1, devices), tile_b], 2)
-    share_w1 = reduce_parts(parts, me, core, devices, (1, 2))
+    share_w1 = reduce_parts(parts, me, core, devices, TURNS)
+    share = spread(jnp.concatenate([share_w2, share_w1], 1), TURNS)
+    share_w2, share_w1 = share[: own * width // 128], share[own * width // 128 :]
     share_w = jnp.stack(
         [unchunk(share_w1[: own * width // 128], own, width), unchunk(share_w2, own, width)]
     )

time: 220 us -> 211 us (0.959)
  the two profiles are of different devices: /device:TPU:0 before, /device:TPU:1 now
where the time goes in v3:
time: 211 us; the launch traced here: 210 us
  blocking collectives  69.4 us (33%)
  local copies, waits for them, and re-layouts  30.7 us (15%)
  waiting for transfers between devices  26 us (12%)
  matrix products  24.7 us (12%)
  Pallas kernels  19.8 us (9%)
  other arithmetic  19.7 us (9%)
  starting transfers between devices  18.5 us (9%)
    all_to_all x1, blocking collectives, chips_all_to_all(): lax.all_to_all(x, AXES, 0, 0, tiled=True, axis_index_groups=chip_groups(d...  43.5 us
    all_to_all x1, blocking collectives, spread(): got = lax.all_to_all(mine, AXES, 0, 0, tiled=True, axis_index_groups=groups)  25.9 us
    ppermute x4, waiting for transfers between devices, halve(): return keep + lax.ppermute(send, AXES, pairs)  24.7 us
    pallas_call x1, Pallas kernels, solve(): pl.pallas_call(solve_kernel, out_shape=(jax.ShapeDtypeStruct(field.shape,...  16 us
    gather x1, local copies, waits for them, and re-layouts, step_all(): stored = reservoir[res_slot]  13.3 us
    ppermute x4, starting transfers between devices, exchange(): return (lax.ppermute(first, axis, down), lax.ppermute(last, axis, up))  9.25 us
    ppermute x4, starting transfers between devices, halve(): return keep + lax.ppermute(send, AXES, pairs)  6.57 us
    add x4, other arithmetic, halve(): return keep + lax.ppermute(send, AXES, pairs)  5.45 us
  transfers between devices with their start and end apart: 11, of which 4 were waited for; matrix products, arithmetic and copies ran while one was open for 16% of the time, Pallas kernels for 9%

profile of v3, /device:TPU:1, one launch (start us, length us, event | category | flops | bytes accessed | tf_op | source)
XLA Modules:
  0.0 209.8 jit_solution(4148380142553547192)
XLA Ops:
  3.3 43.5 %all_to_all.10 = bf16[64,2,8,1152]{3,2,1,0:T(8,128)(2,1)S(1)} all-to-all(bf16[64,2,8,1152]{3,2,1,0:T(8,128)(2,1)S(1)} %broadcast_in_dim.21), channel_id=1, replica_groups={{0,2,4,6,8,10,12,14,16,18,20,22,24,26,28,30,32,34,36,38,40,42,44,46,48,..., dimensions={0} | all-to-all | bytes 4718592 | tf_op jit(solution)/shard_map/all_to_all | solution.py:279
  46.9 1.6 copy.48
  48.5 2.2 %collective-permute-start.4 = (bf16[64,2,8,1152]{3,2,0,1:T(8,128)(2,1)}, bf16[64,2,8,1152]{3,2,0,1:T(8,128)(2,1)}, u32[]{:S(2)}, u32[]{:S(2)}) collective-permute-start(bf16[64,2,8,1152]{3,2,0,1:T(8,128)(2,1)} %copy.48), channel_id=1, source_target_pairs={{0,1},{1,0},{2,3},{3,2},{4,5},{5,4},{6,7},{7,6},{8,9},{9,8},{10,11... | collective-permute-start | bytes 7077896 | tf_op jit(solution)/shard_map/ppermute | solution.py:275
  52.9 2.2 %collective-permute-start.1 = (f32[3,32,4,128]{3,2,1,0:T(4,128)S(1)}, f32[3,32,4,128]{3,2,1,0:T(4,128)S(1)}, u32[]{:S(2)}, u32[]{:S(2)}) collective-permute-start(f32[3,32,4,128]{3,2,1,0:T(4,128)S(1)} %pad_maximum_fusion.5), channel_id=1, source_target_pairs={{0,8},{8,16},{16,24},{24,32},{32,40},{40,48},{48,56},{56,64},{64,7... | collective-permute-start | bytes 589832 | tf_op jit(solution)/shard_map/ppermute | solution.py:29
  55.2 1.3 collective-permute-start
  56.5 13.3 %gather_fusion = bf16[1024,2048]{1,0:T(8,128)(2,1)} fusion(bf16[2048,2048]{1,0:T(8,128)(2,1)} %param.23, s32[1024]{0:T(1024)S(1)} %fusion.11), kind=kCustom, calls=%fused_computation | custom fusion | bytes 8392704 | tf_op jit(solution)/shard_map/gather | solution.py:400
  70.8 3.8 %pack_sides.1 = (f32[3,72,128]{2,1,0:T(8,128)}, f32[3,72,128]{2,1,0:T(8,128)}) custom-call(f32[32,64,128]{2,1,0:T(8,128)} %u_ref.3, f32[32,64,128]{2,1,0:T(8,128)} %k_ref.3, f32[32,64,128]{2,1,0:T(8,128)} %r_ref.3, f32[3,32,8,128]{3,2,1,0:T(8,128)} %pad_maximum_fusion.3.halo_ref), custom_call_target="tpu_custom_call" | custom-call | flops 16777216 | bytes 12582912 | tf_op jit(solution)/shard_map/pack_sides/pallas_call | solution.py:56
  74.5 2.2 %collective-permute-start.2 = (f32[3,72,128]{2,1,0:T(8,128)}, f32[3,72,128]{2,1,0:T(8,128)S(1)}, u32[]{:S(2)}, u32[]{:S(2)}) collective-permute-start(f32[3,72,128]{2,1,0:T(8,128)} %get-tuple-element.35), channel_id=1, source_target_pairs={{1,0},{2,1},{3,2},{4,3},{5,4},{6,5},{7,6},{9,8},{10,9},{11,10},{12... | collective-permute-start | bytes 331784 | tf_op jit(solution)/shard_map/ppermute | solution.py:29
  76.7 3.6 %collective-permute-start.3 = (f32[3,72,128]{2,1,0:T(8,128)}, f32[3,72,128]{2,1,0:T(8,128)S(1)}, u32[]{:S(2)}, u32[]{:S(2)}) collective-permute-start(f32[3,72,128]{2,1,0:T(8,128)} %get-tuple-element.36), channel_id=1, source_target_pairs={{0,1},{1,2},{2,3},{3,4},{4,5},{5,6},{6,7},{8,9},{9,10},{10,11},{11... | collective-permute-start | bytes 331784 | tf_op jit(solution)/shard_map/ppermute | solution.py:29
  80.9 1.3 collective-permute-done.3.left_ref
  82.8 16.0 %solve.1 = (f32[32,64,128]{2,1,0:T(8,128)}, bf16[256,2048]{1,0:T(8,128)(2,1)}) custom-call(s32[4]{0:T(128)} %pad_add_fusion.pos_ref, f32[32,64,128]{2,1,0:T(8,128)} %u_ref.3, f32[32,64,128]{2,1,0:T(8,128)} %k_ref.3, f32[32,64,128]{2,1,0:T(8,128)} %r_ref.3, f32[3,32,8,128]{3,2,1,0:T(8,128)} %pad_maximum_fusion.3.halo_ref, f32[3,72,128]{2,1,0:T(8,128)} %copy-done.9, ...), custom_call_target="tpu_custom_call" | custom-call | flops 125829120 | bytes 67108864 | tf_op jit(solution)/shard_map/solve/pallas_call | solution.py:243
  98.8 2.7 %convolution_convert_fusion = bf16[256,2048]{1,0:T(8,128)(2,1)} fusion(bf16[256,2048]{1,0:T(8,128)(2,1)} %get-tuple-element.38, s32[256]{0:T(256)S(1)} %fusion.14), kind=kOutput, calls=%fused_computation.13 | convolution fusion | flops 269025280 | bytes 2098176 | tf_op jit(solution)/shard_map/dot_general | solution.py:392
  101.5 2.1 select_bitcast_fusion.1
  104.1 2.1 %copy-done.3 = bf16[64,2,2,8,1152]{4,3,1,0,2:T(8,128)(2,1)} copy-done((bf16[64,2,2,8,1152]{4,3,1,0,2:T(8,128)(2,1)}, bf16[64,2,2,8,1152]{4,3,1,0,2:T(8,128)(2,1)S(1)}, u32[]{:S(2)}) %copy-start.3) | copy-done | bytes 4718616
  107.6 5.3 %add_tanh_fusion = f32[1280,1024]{1,0:T(8,128)S(1)} fusion(f32[1024]{0:T(1024)S(1)} %add.136, bf16[2,1024,1152]{2,1,0:T(8,128)(2,1)} %bitcast.121, bf16[1024,2048]{1,0:T(8,128)(2,1)} %gather_fusion, bf16[256,2048]{1,0:T(8,128)(2,1)S(1)} %copy-done.7), kind=kOutput, calls=%fused_computation.5 | convolution fusion | flops 2690908160 | bytes 12587008 | tf_op jit(solution)/shard_map/dot_general | solution.py:405
  113.6 4.2 %fusion.21 = (f32[1024]{0:T(1024)S(1)}, bf16[1280,1024]{1,0:T(8,128)(2,1)S(1)}) fusion(f32[1280]{0:T(1024)S(1)} %pad_divide_fusion, bf16[256,2048]{1,0:T(8,128)(2,1)S(1)} %copy-done.7, bf16[1024,2048]{1,0:T(8,128)(2,1)S(1)} %copy-done.4, f32[1024]{0:T(1024)S(1)} %add.139, bf16[2,1024,1152]{2,1,0:T(8,128)(2,1)S(1)} %bitcast.124, ...), kind=kOutput, calls=%fused_computation.86 | convolution fusion | flops 2697460736 | bytes 15220736 | tf_op jit(solution)/shard_map/dot_general | solution.py:408
  117.8 3.5 %fusion.22 = (f32[1024]{0:T(1024)S(1)}, bf16[1280,1024]{1,0:T(8,128)(2,1)S(1)}) fusion(f32[1280,1024]{1,0:T(8,128)S(1)} %add_tanh_fusion, bf16[2,1024,1152]{2,1,0:T(8,128)(2,1)S(1)} %bitcast.125, bf16[1280,1024]{1,0:T(8,128)(2,1)S(1)} %get-tuple-element.60), kind=kOutput, calls=%fused_computation.87 | convolution fusion | flops 2690907136 | bytes 12587008 | tf_op jit(solution)/shard_map/dot_general | solution.py:413
  121.4 4.5 %fusion.4 = f32[1024,1024]{1,0:T(8,128)} fusion(bf16[1280,1024]{1,0:T(8,128)(2,1)S(1)} %get-tuple-element.60, f32[1280,1024]{1,0:T(8,128)S(1)} %add_tanh_fusion), kind=kOutput, calls=%fused_computation.25 | convolution fusion | flops 2685665280 | bytes 12058624 | tf_op jit(solution)/shard_map/dot_general | solution.py:411
  125.9 4.4 %fusion.1 = f32[1024,1024]{1,0:T(8,128)} fusion(bf16[1280,1024]{1,0:T(8,128)(2,1)S(1)} %get-tuple-element.62, bf16[1024,2048]{1,0:T(8,128)(2,1)S(1)} %copy-done.4, bf16[256,2048]{1,0:T(8,128)(2,1)S(1)} %copy-done.7), kind=kOutput, calls=%fused_computation.11 | convolution fusion | flops 2689597440 | bytes 12058624 | tf_op jit(solution)/shard_map/dot_general | solution.py:417
  130.9 3.3 %dynamic-slice_bitcast_fusion.1 = f32[64,64,128]{2,1,0:T(8,128)} fusion(f32[2,64,64,128]{3,2,0,1:T(8,128)} %bitcast.126, s32[]{:T(128)S(6)} %select_n.99), kind=kLoop, calls=%fused_computation.23 | loop fusion | bytes 4194308 | tf_op jit(solution)/shard_map/jit(dynamic_index_in_dim)/squeeze | solution.py:344
  134.7 2.1 %copy-done = f32[2,64,72,128]{3,2,1,0:T(8,128)} copy-done((f32[2,64,72,128]{3,2,1,0:T(8,128)}, f32[2,64,72,128]{3,2,1,0:T(8,128)S(1)}, u32[]{:S(2)}) %copy-start) | copy-done | bytes 4718616
  136.8 1.7 dynamic-slice_bitcast_fusion
  139.0 2.0 bitcast_add_fusion.1
  142.4 2.8 %collective-permute-start.6 = (f32[2,16,64,128]{3,2,1,0:T(8,128)}, f32[2,16,64,128]{3,2,1,0:T(8,128)}, u32[]{:S(2)}, u32[]{:S(2)}) collective-permute-start(f32[2,16,64,128]{3,2,1,0:T(8,128)} %dynamic-slice_bitcast_fusion.3), channel_id=1, source_target_pairs={{0,96},{1,25},{2,98},{3,27},{4,100},{5,29},{6,102},{7,31},{8,104},... | collective-permute-start | bytes 3145736 | tf_op jit(solution)/shard_map/ppermute | solution.py:329
  145.2 1.9 bitcast_add_fusion
  147.4 2.2 %collective-permute-start.9 = (f32[2,16,72,128]{3,2,1,0:T(8,128)S(1)}, f32[2,16,72,128]{3,2,1,0:T(8,128)}, u32[]{:S(2)}, u32[]{:S(2)}) collective-permute-start(f32[2,16,72,128]{3,2,1,0:T(8,128)S(1)} %dynamic-slice_bitcast_fusion.2), channel_id=1, source_target_pairs={{0,96},{1,25},{2,98},{3,27},{4,100},{5,29},{6,102},{7,31},{8,104},... | collective-permute-start | bytes 3538952 | tf_op jit(solution)/shard_map/ppermute | solution.py:329
  149.6 8.4 %collective-permute-done.6 = f32[2,16,64,128]{3,2,1,0:T(8,128)} collective-permute-done((f32[2,16,64,128]{3,2,1,0:T(8,128)}, f32[2,16,64,128]{3,2,1,0:T(8,128)}, u32[]{:S(2)}, u32[]{:S(2)}) %collective-permute-start.6) | collective-permute-done | bytes 1048608 | tf_op jit(solution)/shard_map/ppermute | solution.py:329
  158.0 1.7 bitcast_add_fusion.3
  161.4 9.2 %collective-permute-done.9 = f32[2,16,72,128]{3,2,1,0:T(8,128)} collective-permute-done((f32[2,16,72,128]{3,2,1,0:T(8,128)S(1)}, f32[2,16,72,128]{3,2,1,0:T(8,128)}, u32[]{:S(2)}, u32[]{:S(2)}) %collective-permute-start.9) | collective-permute-done | bytes 1179680 | tf_op jit(solution)/shard_map/ppermute | solution.py:329
  170.6 1.4 bitcast_add_fusion.2
  174.2 7.1 %collective-permute-done.10 = f32[16,72,128]{2,1,0:T(8,128)} collective-permute-done((f32[16,72,128]{2,1,0:T(8,128)S(1)}, f32[16,72,128]{2,1,0:T(8,128)}, u32[]{:S(2)}, u32[]{:S(2)}) %collective-permute-start.10) | collective-permute-done | bytes 589856 | tf_op jit(solution)/shard_map/ppermute | solution.py:329
  182.6 25.9 %all_to_all.11 = f32[16,136,128]{2,1,0:T(8,128)S(1)} all-to-all(f32[16,136,128]{2,1,0:T(8,128)S(1)} %pad_maximum_fusion.2), channel_id=1, replica_groups={{0,2,4,6,8,10,12,14,16,18,20,22,24,26,28,30},{32,34,36,38,40,42,44,46,4..., dimensions={0} | all-to-all | bytes 2228224 | tf_op jit(solution)/shard_map/all_to_all | solution.py:359
  (99 shorter events, 19.2 us)
Async XLA Ops:
  46.9 9.6 %copy-start.13 = (s32[1024]{0:T(1024)S(1)}, s32[1024]{0:T(1024)}, u32[]{:S(2)}) copy-start(s32[1024]{0:T(1024)} %param.22) | copy-start | bytes 12292
  48.5 53.0 %collective-permute-start.4 = (bf16[64,2,8,1152]{3,2,0,1:T(8,128)(2,1)}, bf16[64,2,8,1152]{3,2,0,1:T(8,128)(2,1)}, u32[]{:S(2)}, u32[]{:S(2)}) collective-permute-start(bf16[64,2,8,1152]{3,2,0,1:T(8,128)(2,1)} %copy.48), channel_id=1, source_target_pairs={{0,1},{1,0},{2,3},{3,2},{4,5},{5,4},{6,7},{7,6},{8,9},{9,8},{10,11... | collective-permute-start | bytes 7077896 | tf_op jit(solution)/shard_map/ppermute | solution.py:275
  52.9 17.0 %collective-permute-start.1 = (f32[3,32,4,128]{3,2,1,0:T(4,128)S(1)}, f32[3,32,4,128]{3,2,1,0:T(4,128)S(1)}, u32[]{:S(2)}, u32[]{:S(2)}) collective-permute-start(f32[3,32,4,128]{3,2,1,0:T(4,128)S(1)} %pad_maximum_fusion.5), channel_id=1, source_target_pairs={{0,8},{8,16},{16,24},{24,32},{32,40},{40,48},{48,56},{56,64},{64,7... | collective-permute-start | bytes 589832 | tf_op jit(solution)/shard_map/ppermute | solution.py:29
  55.2 14.7 %collective-permute-start = (f32[3,32,4,128]{3,2,1,0:T(4,128)S(1)}, f32[3,32,4,128]{3,2,1,0:T(4,128)S(1)}, u32[]{:S(2)}, u32[]{:S(2)}) collective-permute-start(f32[3,32,4,128]{3,2,1,0:T(4,128)S(1)} %pad_maximum_fusion.4), channel_id=1, source_target_pairs={{8,0},{16,8},{24,16},{32,24},{40,32},{48,40},{56,48},{64,56},{72,6... | collective-permute-start | bytes 589832 | tf_op jit(solution)/shard_map/ppermute | solution.py:29
  56.5 13.4 %copy-start.17 = (s32[256]{0:T(256)S(1)}, s32[256]{0:T(256)}, u32[]{:S(2)}) copy-start(s32[256]{0:T(256)} %param.20) | copy-start | bytes 3076
  74.5 6.3 %collective-permute-start.2 = (f32[3,72,128]{2,1,0:T(8,128)}, f32[3,72,128]{2,1,0:T(8,128)S(1)}, u32[]{:S(2)}, u32[]{:S(2)}) collective-permute-start(f32[3,72,128]{2,1,0:T(8,128)} %get-tuple-element.35), channel_id=1, source_target_pairs={{1,0},{2,1},{3,2},{4,3},{5,4},{6,5},{7,6},{9,8},{10,9},{11,10},{12... | collective-permute-start | bytes 331784 | tf_op jit(solution)/shard_map/ppermute | solution.py:29
  76.7 5.4 %collective-permute-start.3 = (f32[3,72,128]{2,1,0:T(8,128)}, f32[3,72,128]{2,1,0:T(8,128)S(1)}, u32[]{:S(2)}, u32[]{:S(2)}) collective-permute-start(f32[3,72,128]{2,1,0:T(8,128)} %get-tuple-element.36), channel_id=1, source_target_pairs={{0,1},{1,2},{2,3},{3,4},{4,5},{5,6},{6,7},{8,9},{9,10},{10,11},{11... | collective-permute-start | bytes 331784 | tf_op jit(solution)/shard_map/ppermute | solution.py:29
  80.9 1.3 copy-start.9
  82.2 0.7 copy-start.10
  103.6 3.7 %copy-start.18 = (s32[256,1]{0,1:T(1,128)S(1)}, s32[256,1]{0,1:T(1,128)}, u32[]{:S(2)}) copy-start(s32[256,1]{0,1:T(1,128)} %param.21) | copy-start | bytes 3076
  103.6 4.0 %copy-start.7 = (bf16[256,2048]{1,0:T(8,128)(2,1)S(1)}, bf16[256,2048]{1,0:T(8,128)(2,1)}, u32[]{:S(2)}) copy-start(bf16[256,2048]{1,0:T(8,128)(2,1)} %convolution_convert_fusion) | copy-start | bytes 3145732
  104.1 2.1 %copy-start.3 = (bf16[64,2,2,8,1152]{4,3,1,0,2:T(8,128)(2,1)}, bf16[64,2,2,8,1152]{4,3,1,0,2:T(8,128)(2,1)S(1)}, u32[]{:S(2)}) copy-start(bf16[64,2,2,8,1152]{4,3,1,0,2:T(8,128)(2,1)S(1)} %pad_maximum_fusion) | copy-start | bytes 14155780
  106.6 7.0 %slice-start = ((s8[4718592]{0:T(1024)(128)(4,1)}), s8[524288]{0:T(1024)(128)(4,1)S(1)}, s32[]{:S(2)}) async-start(s8[4718592]{0:T(1024)(128)(4,1)} %bitcast.122), calls=%async_computation.2 | async-start | bytes 1048576
  107.6 6.0 %slice-start.1 = ((s8[4718592]{0:T(1024)(128)(4,1)}), s8[4194304]{0:T(1024)(128)(4,1)S(1)}, s32[]{:S(2)}) async-start(s8[4718592]{0:T(1024)(128)(4,1)} %bitcast.122), calls=%async_computation.3 | async-start | bytes 8388608
  107.6 6.0 %copy-start.4 = (bf16[1024,2048]{1,0:T(8,128)(2,1)S(1)}, bf16[1024,2048]{1,0:T(8,128)(2,1)}, u32[]{:S(2)}) copy-start(bf16[1024,2048]{1,0:T(8,128)(2,1)} %gather_fusion) | copy-start | bytes 12582916
  130.9 3.4 %copy-start.5 = (f32[1024,1024]{1,0:T(8,128)S(1)}, f32[1024,1024]{1,0:T(8,128)}, u32[]{:S(2)}) copy-start(f32[1024,1024]{1,0:T(8,128)} %fusion.1) | copy-start | bytes 12582916
  134.3 4.8 %collective-permute-start.5 = (f32[64,64,128]{2,1,0:T(8,128)}, f32[64,64,128]{2,1,0:T(8,128)S(1)}, u32[]{:S(2)}, u32[]{:S(2)}) collective-permute-start(f32[64,64,128]{2,1,0:T(8,128)} %dynamic-slice_bitcast_fusion.1), channel_id=1, source_target_pairs={{0,1},{1,0},{2,3},{3,2},{4,5},{5,4},{6,7},{7,6},{8,9},{9,8},{10,11... | collective-permute-start | bytes 6291464 | tf_op jit(solution)/shard_map/ppermute | solution.py:275
  134.7 2.1 %copy-start = (f32[2,64,72,128]{3,2,1,0:T(8,128)}, f32[2,64,72,128]{3,2,1,0:T(8,128)S(1)}, u32[]{:S(2)}) copy-start(f32[2,64,72,128]{3,2,1,0:T(8,128)S(1)} %select_maximum_fusion) | copy-start | bytes 14155780
  138.5 6.6 %collective-permute-start.8 = (f32[64,72,128]{2,1,0:T(8,128)}, f32[64,72,128]{2,1,0:T(8,128)}, u32[]{:S(2)}, u32[]{:S(2)}) collective-permute-start(f32[64,72,128]{2,1,0:T(8,128)} %dynamic-slice_bitcast_fusion), channel_id=1, source_target_pairs={{0,1},{1,0},{2,3},{3,2},{4,5},{5,4},{6,7},{7,6},{8,9},{9,8},{10,11... | collective-permute-start | bytes 7077896 | tf_op jit(solution)/shard_map/ppermute | solution.py:275
  141.0 4.1 %copy-start.1 = (f32[2,64,72,128]{3,2,1,0:T(8,128)S(1)}, f32[2,64,72,128]{3,2,1,0:T(8,128)}, u32[]{:S(2)}) copy-start(f32[2,64,72,128]{3,2,1,0:T(8,128)} %copy-done) | copy-start | bytes 14155780
  141.2 3.9 %copy-start.2 = (f32[4,4,4,64,128]{4,3,2,1,0:T(8,128)}, f32[4,4,4,64,128]{4,3,2,1,0:T(8,128)S(1)}, u32[]{:S(2)}) copy-start(f32[4,4,4,64,128]{4,3,2,1,0:T(8,128)S(1)} %bitcast_select_fusion.1) | copy-start | bytes 6291460
  142.4 15.6 %collective-permute-start.6 = (f32[2,16,64,128]{3,2,1,0:T(8,128)}, f32[2,16,64,128]{3,2,1,0:T(8,128)}, u32[]{:S(2)}, u32[]{:S(2)}) collective-permute-start(f32[2,16,64,128]{3,2,1,0:T(8,128)} %dynamic-slice_bitcast_fusion.3), channel_id=1, source_target_pairs={{0,96},{1,25},{2,98},{3,27},{4,100},{5,29},{6,102},{7,31},{8,104},... | collective-permute-start | bytes 3145736 | tf_op jit(solution)/shard_map/ppermute | solution.py:329
  147.4 23.2 %collective-permute-start.9 = (f32[2,16,72,128]{3,2,1,0:T(8,128)S(1)}, f32[2,16,72,128]{3,2,1,0:T(8,128)}, u32[]{:S(2)}, u32[]{:S(2)}) collective-permute-start(f32[2,16,72,128]{3,2,1,0:T(8,128)S(1)} %dynamic-slice_bitcast_fusion.2), channel_id=1, source_target_pairs={{0,96},{1,25},{2,98},{3,27},{4,100},{5,29},{6,102},{7,31},{8,104},... | collective-permute-start | bytes 3538952 | tf_op jit(solution)/shard_map/ppermute | solution.py:329
  159.7 1.7 copy-start.6
  160.6 12.3 %collective-permute-start.7 = (f32[16,64,128]{2,1,0:T(8,128)}, f32[16,64,128]{2,1,0:T(8,128)}, u32[]{:S(2)}, u32[]{:S(2)}) collective-permute-start(f32[16,64,128]{2,1,0:T(8,128)} %dynamic-slice_bitcast_fusion.5), channel_id=1, source_target_pairs={{0,32},{1,9},{2,34},{3,11},{4,36},{5,13},{6,38},{7,15},{8,40},{9,1... | collective-permute-start | bytes 1572872 | tf_op jit(solution)/shard_map/ppermute | solution.py:329
  172.1 9.2 %collective-permute-start.10 = (f32[16,72,128]{2,1,0:T(8,128)S(1)}, f32[16,72,128]{2,1,0:T(8,128)}, u32[]{:S(2)}, u32[]{:S(2)}) collective-permute-start(f32[16,72,128]{2,1,0:T(8,128)S(1)} %dynamic-slice_bitcast_fusion.4), channel_id=1, source_target_pairs={{0,32},{1,9},{2,34},{3,11},{4,36},{5,13},{6,38},{7,15},{8,40},{9,1... | collective-permute-start | bytes 1769480 | tf_op jit(solution)/shard_map/ppermute | solution.py:329
  182.4 26.1 %copy-start.14 = (f32[2,8]{1,0:T(2,128)S(1)}, f32[2,8]{1,0:T(2,128)}, u32[]{:S(2)}) copy-start(f32[2,8]{1,0:T(2,128)} %param.27) | copy-start | bytes 196
  182.4 26.1 %copy-start.15 = (f32[2,8]{1,0:T(2,128)S(1)}, f32[2,8]{1,0:T(2,128)}, u32[]{:S(2)}) copy-start(f32[2,8]{1,0:T(2,128)} %param.28) | copy-start | bytes 196
  182.4 26.1 %copy-start.16 = (f32[2,8]{1,0:T(2,128)S(1)}, f32[2,8]{1,0:T(2,128)}, u32[]{:S(2)}) copy-start(f32[2,8]{1,0:T(2,128)} %param.29) | copy-start | bytes 196
  182.4 26.7 %copy-start.8 = (f32[2,8,1024]{2,1,0:T(8,128)S(1)}, f32[2,8,1024]{2,1,0:T(8,128)}, u32[]{:S(2)}) copy-start(f32[2,8,1024]{2,1,0:T(8,128)} %param.24) | copy-start | bytes 196612
  182.5 26.7 %copy-start.11 = (f32[2,8,1024]{2,1,0:T(8,128)S(1)}, f32[2,8,1024]{2,1,0:T(8,128)}, u32[]{:S(2)}) copy-start(f32[2,8,1024]{2,1,0:T(8,128)} %param.25) | copy-start | bytes 196612
  182.5 26.7 %copy-start.12 = (f32[2,8,1024]{2,1,0:T(8,128)S(1)}, f32[2,8,1024]{2,1,0:T(8,128)}, u32[]{:S(2)}) copy-start(f32[2,8,1024]{2,1,0:T(8,128)} %param.26) | copy-start | bytes 196612
